TPU v7x, 256 devices: a whole 4x4x8 slice. The times are simulated.
256 devices in a mesh: segment: 32 (over z, y), tensor: 8 (over x, core).
Axes of the slice: x: 4, y: 4, z: 8, core: 2. Of those that a mesh axis runs over, the one named last changes fastest.
Arguments:
- x_in: bfloat16 [128, 8192], P(None, 'tensor'), may hold values from -6 to 6
- neighbour_ids: int32 [512], replicated, may hold values from 0 to 65535
- embed_table: bfloat16 [65536, 896], P(('segment', 'tensor')), may hold values from -6 to 6
- enc_gate: bfloat16 [896, 3584], P(None, 'tensor'), may hold values from -0.1875 to 0.1875
- enc_up: bfloat16 [896, 3584], P(None, 'tensor'), may hold values from -0.1875 to 0.1875
- enc_down: bfloat16 [3584, 896], P('tensor'), may hold values from -0.09375 to 0.09375
- query_weight: bfloat16 [32, 8192, 2048], P('segment', 'tensor'), may hold values from -0.0625 to 0.0625
- key_weight: bfloat16 [32, 896, 2048], P('segment', None, 'tensor'), may hold values from -0.1875 to 0.1875
- value_weight: bfloat16 [32, 896, 2048], P('segment', None, 'tensor'), may hold values from -0.1875 to 0.1875
- out_weight: bfloat16 [32, 2048, 8192], P('segment', None, 'tensor'), may hold values from -0.125 to 0.125
- state_grad: bfloat16 [32, 128, 8192], P('segment', None, 'tensor'), may hold values from -6 to 6
Outputs:
- section_states: bfloat16 [32, 128, 8192], P('segment', None, 'tensor')
- enc_grad: float32 [512, 896], P(('segment', 'tensor'))
All inputs are finite; a program needn't handle non-finite values.
Results may differ from a plain program's by a relative error of at most 0.03.
Values may be sent and summed in bfloat16 or wider, within the bound.
No kernel may reach another device: no remote copies, remote signals or barrier semaphores. Data moves between devices by JAX's collectives and lax.ppermute only.
A program may use at most 64 MiB of HBM per device.

v0:
```python
import functools
import math

import jax
import jax.numpy as jnp
from jax import lax
from jax.experimental import pallas as pl
from jax.experimental.pallas import tpu as pltpu
from jax.sharding import Mesh
from jax.sharding import PartitionSpec as P


HD = 64
SPAN = 64
Z, Y, X, C = "segment_0", "segment_1", "tensor_0", "tensor_1"
SEGMENT = (Z, Y)
TENSOR = (X, C)
SEGMENT_TENSOR = (Z, Y, X, C)

EPSILON = 1e-06
SCORE_GAIN = 2.0
F32 = jnp.float32
BF16 = jnp.bfloat16


NT = (((1,), (1,)), ((), ()))
TN = (((0,), (0,)), ((), ()))
NN = (((1,), (0,)), ((), ()))

PARAMS = pltpu.CompilerParams(vmem_limit_bytes=24 << 20)


def swap(value, axis, k):
    size = lax.axis_size(axis)
    return lax.ppermute(value, axis, [(i, i ^ k) for i in range(size)])


def dot(lhs, rhs, dims=NN):
    return lax.dot_general(lhs, rhs, dims, preferred_element_type=F32)


def halves(value):
    high = value.astype(BF16)
    return high, (value - high.astype(F32)).astype(BF16)


def head_of(shape, dim):
    return lax.broadcasted_iota(jnp.int32, shape, dim) // HD


def head_mean(value):
    width = value.shape[-1]
    same = head_of((width, width), 0) == head_of((width, width), 1)
    mean = jnp.where(same, 1.0 / HD, 0.0).astype(BF16)
    high, low = halves(value)
    return dot(high, mean) + dot(low, mean)


def by_head(rows):
    heads = rows.shape[-1] // HD
    which = head_of(rows.shape, 1)
    return jnp.concatenate([jnp.where(which == h, rows, 0.0) for h in range(heads)], axis=0)


def project_kernel(index_ref, x_ref, wq_ref, grad_ref, wo_ref, out_ref, q_buf, o_buf, sem, *, other_core):
    copies = []
    for k in range(4):
        start = pl.multiple_of((index_ref[0] ^ (2 * k + other_core)) * 256, 256)
        copies.append(
            (
                pltpu.make_async_copy(wq_ref.at[:, pl.ds(start, 256)], q_buf.at[k], sem.at[0, k]),
                pltpu.make_async_copy(wo_ref.at[pl.ds(start, 256), :], o_buf.at[k], sem.at[1, k]),
            )
        )
        for copy in copies[k]:
            copy.start()
    for k in range(4):
        for copy in copies[k]:
            copy.wait()
        out_ref[k, 0] = dot(x_ref[...], q_buf[k]).astype(BF16)
        out_ref[k, 1] = dot(grad_ref[...], o_buf[k], NT).astype(BF16)


def project(index, x_in, w_query, grad, w_out, other_core):
    tokens, depth = x_in.shape
    shape = (4, 2, tokens, 256)
    anywhere = pl.BlockSpec(memory_space=pltpu.HBM)
    return pl.pallas_call(
        functools.partial(project_kernel, other_core=other_core),
        out_shape=jax.ShapeDtypeStruct(shape, BF16),
        in_specs=[
            pl.BlockSpec(memory_space=pltpu.SMEM),
            whole((tokens, depth)),
            anywhere,
            whole((tokens, depth)),
            anywhere,
        ],
        out_specs=whole(shape),
        scratch_shapes=[
            pltpu.VMEM((4, depth, 256), BF16),
            pltpu.VMEM((4, 256, depth), BF16),
            pltpu.SemaphoreType.DMA((2, 4)),
        ],
        cost_estimate=pl.CostEstimate(
            flops=16 * tokens * depth * 256, bytes_accessed=16 * depth * 256, transcendentals=0
        ),
        compiler_params=PARAMS,
        name="project",
    )(index, x_in, w_query, grad, w_out)


def attend_kernel(own_ref, oth_ref, wk_ref, wv_ref, heads_ref, att_ref,
                  key_ref, val_ref, weight_ref, qhat_ref):
    wk = wk_ref[...]
    wv = wv_ref[...]
    query = heads_ref[0]
    query = query * lax.rsqrt(head_mean(query * query) + EPSILON)
    qhat_ref[...] = query.astype(BF16)
    for span in range(2):
        enc = jnp.concatenate([own_ref[span], oth_ref[span]], axis=0)
        key = dot(enc, wk)
        value = dot(enc, wv).astype(BF16)
        key_ref[span] = key
        val_ref[span] = value
        khat = key * lax.rsqrt(head_mean(key * key) + EPSILON)
        q_high, q_low = halves(by_head(query[span * SPAN : (span + 1) * SPAN]))
        k_high, k_low = halves(khat)
        score = dot(q_high, k_high, NT) + dot(q_high, k_low, NT) + dot(q_low, k_high, NT)
        weight = jnp.exp(score * (SCORE_GAIN / math.sqrt(HD)))
        weight = weight / jnp.sum(weight, axis=-1, keepdims=True)
        weight_ref[span] = weight
        mixed = dot(weight.astype(BF16), value)
        which = head_of((SPAN, 256), 1)
        out = jnp.zeros((SPAN, 256), F32)
        for h in range(4):
            out = jnp.where(which == h, mixed[h * SPAN : (h + 1) * SPAN], out)
        att_ref[span * SPAN : (span + 1) * SPAN] = out.astype(BF16)


def whole(shape):
    return pl.BlockSpec(shape, lambda: (0,) * len(shape))


def attend(own, oth, w_key, w_value, heads):
    depth = w_key.shape[0]
    piece = whole((2, 128, 256))
    shapes = [((128, 256), BF16), ((2, 256, 256), F32), ((2, 256, 256), BF16),
              ((2, 256, 256), F32), ((128, 256), BF16)]
    return pl.pallas_call(
        attend_kernel,
        out_shape=[jax.ShapeDtypeStruct(*s) for s in shapes],
        in_specs=[whole((2, 128, depth))] * 2 + [whole((depth, 256))] * 2 + [piece],
        out_specs=[whole(s[0]) for s in shapes],
        cost_estimate=pl.CostEstimate(
            flops=4 * 512 * depth * 256, bytes_accessed=4 * 512 * depth, transcendentals=131072
        ),
        compiler_params=PARAMS,
        name="attend",
    )(own, oth, w_key, w_value, heads)


def backward_kernel(x_ref, heads_ref, key_ref, val_ref, weight_ref, qhat_ref, wk_ref, wv_ref,
                    keep_ref, send_ref):
    wk = wk_ref[...]
    wv = wv_ref[...]
    grad = heads_ref[1]
    for span in range(2):
        rows = slice(span * SPAN, (span + 1) * SPAN)
        d_out = by_head(grad[rows]).astype(BF16)
        q_rows = by_head(qhat_ref[rows].astype(F32)).astype(BF16)
        weight = weight_ref[span]
        value = val_ref[span]
        d_value = dot(weight.astype(BF16), d_out, TN).astype(BF16)
        d_weight = dot(d_out, value, NT)
        d_score = weight * (d_weight - jnp.sum(weight * d_weight, axis=-1, keepdims=True))
        d_khat = dot(d_score.astype(BF16), q_rows, TN) * (SCORE_GAIN / math.sqrt(HD))
        key = key_ref[span]
        scale = lax.rsqrt(head_mean(key * key) + EPSILON)
        khat = key * scale
        d_key = (scale * (d_khat - khat * head_mean(d_khat * khat))).astype(BF16)
        term = dot(d_key, wk, NT) + dot(d_value, wv, NT)
        for block in range(4):
            place = x_ref[0] ^ block
            keep_ref[place, span] = term[block * 32 : (block + 1) * 32].astype(BF16)
            send_ref[place, span] = term[128 + block * 32 : 128 + (block + 1) * 32].astype(BF16)


def backward(x_index, heads, saved, w_key, w_value):
    depth = w_key.shape[0]
    piece = whole((2, 128, 256))
    key, value, weight, qhat = saved
    return pl.pallas_call(
        backward_kernel,
        out_shape=[jax.ShapeDtypeStruct((4, 2, 32, depth), BF16)] * 2,
        in_specs=[pl.BlockSpec(memory_space=pltpu.SMEM)] + [piece]
        + [whole((2, 256, 256))] * 3 + [whole((128, 256))] + [whole((depth, 256))] * 2,
        out_specs=[whole((4, 2, 32, depth))] * 2,
        cost_estimate=pl.CostEstimate(
            flops=4 * 512 * depth * 256, bytes_accessed=4 * 512 * depth, transcendentals=0
        ),
        compiler_params=PARAMS,
        name="backward",
    )(x_index, heads, key, value, weight, qhat, w_key, w_value)


def output_kernel(index_ref, att_ref, wo_ref, *refs, other_core):
    base_ref = refs[0] if other_core else None
    out_ref, buf_ref, sem = refs[-3:]
    copies = []
    for k in range(4):
        row = pl.multiple_of((index_ref[0] ^ (2 * k + other_core)) * 256, 256)
        copies.append(
            pltpu.make_async_copy(
                wo_ref.at[pl.ds(row, 256), :], buf_ref.at[pl.ds(k * 256, 256), :], sem.at[k]
            )
        )
        copies[k].start()
    att = jnp.concatenate([att_ref[k] for k in range(4)], axis=1)
    for copy in copies:
        copy.wait()
    for column in range(4):
        lanes = slice(column * 256, (column + 1) * 256)
        part = dot(att, buf_ref[:, lanes])
        if not other_core:
            out_ref[:, lanes] = part
            continue
        part = (base_ref[:, lanes] + part).astype(BF16)
        half, lane = divmod(column * 256, 512)
        for block in range(16):
            out_ref[2 * block + half, :, lane : lane + 256] = part[block * 8 : (block + 1) * 8]


def output(index, att, w_out, base):
    width = w_out.shape[1]
    second = base is not None
    shape, dtype = ((32, 8, 512), BF16) if second else ((128, width), F32)
    return pl.pallas_call(
        functools.partial(output_kernel, other_core=int(second)),
        out_shape=jax.ShapeDtypeStruct(shape, dtype),
        in_specs=[
            pl.BlockSpec(memory_space=pltpu.SMEM),
            whole((4, 128, 256)),
            pl.BlockSpec(memory_space=pl.ANY),
        ]
        + ([whole((128, width))] if second else []),
        out_specs=whole(shape),
        scratch_shapes=[pltpu.VMEM((1024, width), BF16), pltpu.SemaphoreType.DMA((4,))],
        cost_estimate=pl.CostEstimate(
            flops=2 * 128 * 1024 * width, bytes_accessed=2 * 1024 * width, transcendentals=0
        ),
        compiler_params=PARAMS,
        name="output",
    )(index, att, w_out, *([base] if second else []))


def lookup_kernel(index_ref, ids_ref, table_ref, own_ref, oth_ref):
    core = index_ref[0]
    ids = ids_ref[...] - index_ref[1]
    depth, count = table_ref.shape[0], ids.shape[1]
    hot = jnp.where(lax.broadcasted_iota(jnp.int32, (depth, count), 0) == ids, 1.0, 0.0).astype(BF16)
    source = lax.broadcasted_iota(jnp.int32, (count, count // 2), 0)
    place = lax.broadcasted_iota(jnp.int32, (count, count // 2), 1)
    token = ((place >> 7) << 8) + (((place >> 1) & 15) << 4) + (((place >> 5) & 3) << 2) + (place & 1)
    for out_ref, which in ((oth_ref, 1 - core), (own_ref, core)):
        pick = jnp.where(source == token + 2 * which, 1.0, 0.0).astype(BF16)
        out_ref[...] = dot(dot(hot, pick).astype(BF16), table_ref[...], TN).astype(BF16)


def lookup(index, ids, table):
    shape = (ids.shape[1] // 2, table.shape[1])
    return pl.pallas_call(
        lookup_kernel,
        out_shape=[jax.ShapeDtypeStruct(shape, BF16)] * 2,
        in_specs=[pl.BlockSpec(memory_space=pltpu.SMEM), whole(ids.shape), whole(table.shape)],
        out_specs=[whole(shape)] * 2,
        cost_estimate=pl.CostEstimate(
            flops=4 * 256 * 256 * 896, bytes_accessed=4 * 512 * 896, transcendentals=0
        ),
        compiler_params=PARAMS,
        name="lookup",
    )(index, ids, table)


def encode_kernel(own_ref, oth_ref, gate_ref, up_ref, down_ref, keep_ref, send_ref):
    rows = jnp.concatenate([own_ref[...], oth_ref[...]], axis=0)
    gate = dot(rows, gate_ref[...], NT)
    hidden = (gate / (1.0 + jnp.exp(-gate)) * dot(rows, up_ref[...], NT)).astype(BF16)
    partial = dot(hidden, down_ref[...])
    keep_ref[...] = partial[:8]
    send_ref[...] = partial[8:].astype(BF16)


def encode(own, oth, enc_gate, enc_up, enc_down):
    operands = (own, oth, enc_gate.T, enc_up.T, enc_down)
    return pl.pallas_call(
        encode_kernel,
        out_shape=[jax.ShapeDtypeStruct(own.shape, F32), jax.ShapeDtypeStruct(own.shape, BF16)],
        in_specs=[whole(o.shape) for o in operands],
        out_specs=[whole(own.shape)] * 2,
        cost_estimate=pl.CostEstimate(
            flops=6 * 16 * 896 * 448, bytes_accessed=6 * 896 * 448, transcendentals=8192
        ),
        compiler_params=PARAMS,
        name="encode",
    )(*operands)


def pack_kernel(t0, t1, t2, t3, out_ref, term_ref, wide_ref):
    for chunk in range(7):
        lanes = slice(chunk * 128, (chunk + 1) * 128)
        term_ref[chunk] = sum(t[:, lanes].astype(F32) for t in (t0, t1, t2, t3))
    wide_ref[...] = jnp.zeros_like(wide_ref)
    for chunk in range(7):
        for row in range(2):
            wide_ref[:, chunk, row * 128 : (row + 1) * 128] = term_ref[
                chunk, pl.ds(row, 32, stride=2), :
            ]
    out_ref[...] = wide_ref[...].astype(BF16)


def pack(terms):
    shape = (32, 8, 256)
    return pl.pallas_call(
        pack_kernel,
        out_shape=jax.ShapeDtypeStruct(shape, BF16),
        in_specs=[whole((64, 896))] * 4,
        out_specs=whole(shape),
        scratch_shapes=[pltpu.VMEM((7, 64, 128), F32), pltpu.VMEM(shape, F32)],
        cost_estimate=pl.CostEstimate(flops=262144, bytes_accessed=589824, transcendentals=0),
        compiler_params=PARAMS,
        name="pack",
    )(*terms)


def scan_kernel(_, x_ref, piece_ref, packed_ref, out_ref):
    running = jnp.zeros((8, 512), F32)
    start = x_ref[...].astype(F32)
    for section in range(piece_ref.shape[0]):
        running = running + piece_ref[section].astype(F32)
        out_ref[section, :, :512] = (start + running).astype(BF16)
        out_ref[section, :, 512:] = packed_ref[section]


def scan(index, x_in, pieces, packed):
    return pl.pallas_call(
        scan_kernel,
        out_shape=jax.ShapeDtypeStruct((32, 8, 768), BF16),
        grid_spec=pltpu.PrefetchScalarGridSpec(
            num_scalar_prefetch=1,
            grid=(1,),
            in_specs=[
                pl.BlockSpec((8, 512), lambda i, s: (s[0] // 2, s[0] % 2)),
                pl.BlockSpec((32, 8, 512), lambda i, s: (0, 0, 0)),
                pl.BlockSpec((32, 8, 256), lambda i, s: (0, 0, 0)),
            ],
            out_specs=pl.BlockSpec((32, 8, 768), lambda i, s: (0, 0, 0)),
        ),
        cost_estimate=pl.CostEstimate(flops=262144, bytes_accessed=786432, transcendentals=0),
        compiler_params=PARAMS,
        name="scan",
    )(index, x_in, pieces, packed)


def finish_kernel(in_ref, states_ref, grad_ref):
    for block in range(16):
        for half in range(2):
            states_ref[0, block * 8 : (block + 1) * 8, half * 512 : (half + 1) * 512] = in_ref[
                2 * block + half, :, :512
            ]
    total = in_ref[0, :, 512:].astype(F32)
    for section in range(1, in_ref.shape[0]):
        total = total + in_ref[section, :, 512:].astype(F32)
    for chunk in range(7):
        for row in range(2):
            grad_ref[row : row + 1, chunk * 128 : (chunk + 1) * 128] = total[
                chunk : chunk + 1, row * 128 : (row + 1) * 128
            ]


def finish(arrived):
    shapes = [((1, 128, 1024), BF16), ((2, 896), F32)]
    return pl.pallas_call(
        finish_kernel,
        out_shape=[jax.ShapeDtypeStruct(*s) for s in shapes],
        in_specs=[whole(arrived.shape)],
        out_specs=[whole(s[0]) for s in shapes],
        cost_estimate=pl.CostEstimate(flops=131072, bytes_accessed=786432, transcendentals=0),
        compiler_params=PARAMS,
        name="finish",
    )(arrived)


def gathered_sum(value, keep=None):
    parts = [swap(value, X, k) for k in (1, 2, 3)]
    total = value.astype(F32) if keep is None else keep
    return total + sum(p.astype(F32) for p in parts)


def step(
    x_in,
    neighbour_ids,
    embed_table,
    enc_gate,
    enc_up,
    enc_down,
    query_weight,
    key_weight,
    value_weight,
    out_weight,
    state_grad,
):
    sections = lax.axis_size(SEGMENT)
    section = lax.axis_index(SEGMENT).astype(jnp.int32)
    tensor = lax.axis_index(TENSOR).astype(jnp.int32)
    core = lax.axis_index(C)
    x_index = lax.axis_index(X).astype(jnp.int32)[None]
    t_index = tensor[None]
    s_index = section[None]
    vocab_rows, depth = embed_table.shape
    first_row = (section * lax.axis_size(TENSOR) + tensor) * vocab_rows

    found, passed = lookup(jnp.stack([core.astype(jnp.int32), first_row]), neighbour_ids[None], embed_table)
    paired = (found + swap(passed, C, 1)).reshape(sections, 8, depth)
    w_query, w_key, w_value, w_out = query_weight[0], key_weight[0], value_weight[0], out_weight[0]
    grad_local = state_grad[0]
    own = lax.all_to_all(paired, SEGMENT, 0, 0, tiled=True)
    sent = project(t_index, x_in, w_query, grad_local, w_out, 1)
    sent = swap(sent, C, 1)
    kept = project(t_index, x_in, w_query, grad_local, w_out, 0)
    both = (kept.astype(F32) + sent.astype(F32)).astype(BF16)
    own, both = lax.optimization_barrier((own, both))
    pieces = [both[0]] + [swap(both[k], X, k) for k in (1, 2, 3)]
    heads = sum(p.astype(F32) for p in pieces)

    own = jnp.sum(own.astype(F32), axis=0).astype(BF16)
    own = gathered_sum(own).astype(BF16)
    keep, send = encode(own, swap(own, C, 1), enc_gate, enc_up, enc_down)
    partial = (keep + swap(send, C, 1).astype(F32)).astype(BF16)
    resid = own.astype(F32) + gathered_sum(partial)
    encoding = (
        resid * lax.rsqrt(jnp.mean(resid * resid, axis=-1, keepdims=True) + EPSILON)
    ).astype(BF16)
    enc_own = lax.all_to_all(
        jnp.broadcast_to(encoding[None], (sections, 8, depth)), SEGMENT, 0, 0, tiled=True
    )
    enc_own = enc_own.reshape(2, 128, depth)
    enc_oth = swap(enc_own, C, 1)

    att, *saved = attend(enc_own, enc_oth, w_key, w_value, heads)
    atts = jnp.stack([att] + [swap(att, X, k) for k in (1, 2, 3)])
    keep, send = backward(x_index, heads, saved, w_key, w_value)
    atts_other = swap(atts, C, 1)
    first = output(t_index, atts, w_out, None)
    contribution = output(t_index, atts_other, w_out, first)
    contributions = lax.all_to_all(contribution, SEGMENT, 0, 0, tiled=True)
    terms = (keep.astype(F32) + swap(send, C, 1).astype(F32)).astype(BF16).reshape(4, 64, depth)
    packed = pack([terms[0]] + [swap(terms[k], X, k) for k in (1, 2, 3)])
    mixed = lax.all_to_all(scan(s_index, x_in, contributions, packed), SEGMENT, 0, 0, tiled=True)
    states, enc_grad = finish(mixed)
    return states, enc_grad


def solution(mesh):
    split = Mesh(mesh.devices.reshape(8, 4, 4, 2), SEGMENT_TENSOR)
    return jax.shard_map(
        step,
        mesh=split,
        in_specs=(
            P(None, TENSOR),
            P(),
            P(SEGMENT_TENSOR, None),
            P(None, TENSOR),
            P(None, TENSOR),
            P(TENSOR, None),
            P(SEGMENT, TENSOR, None),
            P(SEGMENT, None, TENSOR),
            P(SEGMENT, None, TENSOR),
            P(SEGMENT, None, TENSOR),
            P(SEGMENT, None, TENSOR),
        ),
        out_specs=(P(SEGMENT, None, TENSOR), P(SEGMENT_TENSOR, None)),
        check_vma=False,
    )
```

profile of v0, /device:TPU:2, one launch (start us, length us, event | category | flops | bytes accessed | tf_op | source)
XLA Modules:
  0.0 137.4 jit_solution(5251679369777401524)
XLA Ops:
  4.1 1.8 %collective-permute-done = bf16[256,896]{1,0:T(8,128)(2,1)S(1)} collective-permute-done((bf16[256,896]{1,0:T(8,128)(2,1)S(1)}, bf16[256,896]{1,0:T(8,128)(2,1)S(1)}, u32[]{:S(2)}, u32[]{:S(2)}) %collective-permute-start) | collective-permute-done | bytes 458784 | tf_op jit(solution)/shard_map/ppermute | solution.py:35
  6.8 11.6 %all-to-all-start = ((bf16[32,8,896]{2,1,0:T(8,128)(2,1)}), bf16[32,8,896]{2,1,0:T(8,128)(2,1)}, u32[]{:S(2)}, u32[]{:S(2)}) async-start(bf16[32,8,896]{2,1,0:T(8,128)(2,1)} %add_bitcast_fusion), calls=%async_computation | async-start | bytes 917504 | tf_op jit(solution)/shard_map/all_to_all | solution.py:426
  18.4 2.2 %copy-done = bf16[1,2048,1024]{2,1,0:T(8,128)(2,1)S(1)} copy-done((bf16[1,2048,1024]{2,1,0:T(8,128)(2,1)S(1)}, bf16[1,2048,1024]{2,1,0:T(8,128)(2,1)}, u32[]{:S(2)}) %copy-start) | copy-done | bytes 4194328
  20.6 2.2 %copy-done.2 = bf16[1,1024,2048]{2,1,0:T(8,128)(2,1)S(1)} copy-done((bf16[1,1024,2048]{2,1,0:T(8,128)(2,1)S(1)}, bf16[1,1024,2048]{2,1,0:T(8,128)(2,1)}, u32[]{:S(2)}) %copy-start.2) | copy-done | bytes 4194328
  24.6 2.5 %project.3 = bf16[4,2,128,256]{3,2,1,0:T(8,128)(2,1)S(1)} custom-call(s32[1]{0:T(128)} %bitcast.1.index_ref, bf16[128,1024]{1,0:T(8,128)(2,1)S(1)} %copy-done.3, bf16[1024,2048]{1,0:T(8,128)(2,1)S(1)} %bitcast.37, bf16[128,1024]{1,0:T(8,128)(2,1)S(1)} %bitcast.45, bf16[2048,1024]{1,0:T(8,128)(2,1)S(1)} %bitcast.33), custom_call_target="tpu_custom_call" | custom-call | flops 536870912 | bytes 4194304 | tf_op jit(solution)/shard_map/project/pallas_call | solution.py:88
  27.3 2.6 %project.2 = bf16[4,2,128,256]{3,2,1,0:T(8,128)(2,1)S(1)} custom-call(s32[1]{0:T(128)} %bitcast.1.index_ref, bf16[128,1024]{1,0:T(8,128)(2,1)S(1)} %copy-done.3, bf16[1024,2048]{1,0:T(8,128)(2,1)S(1)} %bitcast.38, bf16[128,1024]{1,0:T(8,128)(2,1)S(1)} %bitcast.46, bf16[2048,1024]{1,0:T(8,128)(2,1)S(1)} %bitcast.34), custom_call_target="tpu_custom_call" | custom-call | flops 536870912 | bytes 4194304 | tf_op jit(solution)/shard_map/project/pallas_call | solution.py:88
  30.9 4.3 %all-to-all-done = bf16[32,8,896]{2,1,0:T(8,128)(2,1)} async-done(((bf16[32,8,896]{2,1,0:T(8,128)(2,1)}), bf16[32,8,896]{2,1,0:T(8,128)(2,1)}, u32[]{:S(2)}, u32[]{:S(2)}) %all-to-all-start) | async-done | bytes 458784 | tf_op jit(solution)/shard_map/all_to_all | solution.py:426
  40.5 2.6 %collective-permute-done.3 = bf16[8,896]{1,0:T(8,128)(2,1)S(1)} collective-permute-done((bf16[8,896]{1,0:T(8,128)(2,1)S(1)}, bf16[8,896]{1,0:T(8,128)(2,1)S(1)}, u32[]{:S(2)}, u32[]{:S(2)}) %collective-permute-start.3) | collective-permute-done | bytes 14368 | tf_op jit(solution)/shard_map/ppermute | solution.py:35
  46.4 1.8 %collective-permute-start.9 = (bf16[8,896]{1,0:T(8,128)(2,1)S(1)}, bf16[8,896]{1,0:T(8,128)(2,1)S(1)}, u32[]{:S(2)}, u32[]{:S(2)}) collective-permute-start(bf16[8,896]{1,0:T(8,128)(2,1)S(1)} %add_convert_fusion.2), channel_id=1, source_target_pairs={{0,6},{2,4},{4,2},{6,0},{1,7},{3,5},{5,3},{7,1},{8,14},{10,12},{12... | collective-permute-start | bytes 43016 | tf_op jit(solution)/shard_map/ppermute | solution.py:35
  48.3 2.1 %collective-permute-start.8 = (bf16[8,896]{1,0:T(8,128)(2,1)S(1)}, bf16[8,896]{1,0:T(8,128)(2,1)S(1)}, u32[]{:S(2)}, u32[]{:S(2)}) collective-permute-start(bf16[8,896]{1,0:T(8,128)(2,1)S(1)} %add_convert_fusion.2), channel_id=1, source_target_pairs={{0,4},{2,6},{4,0},{6,2},{1,5},{3,7},{5,1},{7,3},{8,12},{10,14},{12... | collective-permute-start | bytes 43016 | tf_op jit(solution)/shard_map/ppermute | solution.py:35
  50.6 2.9 %collective-permute-done.8 = bf16[8,896]{1,0:T(8,128)(2,1)S(1)} collective-permute-done((bf16[8,896]{1,0:T(8,128)(2,1)S(1)}, bf16[8,896]{1,0:T(8,128)(2,1)S(1)}, u32[]{:S(2)}, u32[]{:S(2)}) %collective-permute-start.8) | collective-permute-done | bytes 14368 | tf_op jit(solution)/shard_map/ppermute | solution.py:35
  54.4 20.6 %all_to_all.20 = bf16[32,8,896]{2,1,0:T(8,128)(2,1)S(1)} all-to-all(bf16[32,8,896]{2,1,0:T(8,128)(2,1)S(1)} %broadcast_in_dim.22), channel_id=1, replica_groups=mesh['segment_0'=8,'segment_1'=4,'tensor_0'=4,'tensor_1'=2] {'segment_0'..., dimensions={0} | all-to-all | bytes 917504 | tf_op jit(solution)/shard_map/all_to_all | solution.py:443
  77.4 1.9 %collective-permute-start.12 = (bf16[2,128,256]{2,1,0:T(8,128)(2,1)S(1)}, bf16[2,128,256]{2,1,0:T(8,128)(2,1)S(1)}, u32[]{:S(2)}, u32[]{:S(2)}) collective-permute-start(bf16[2,128,256]{2,1,0:T(8,128)(2,1)S(1)} %get-tuple-element.30), channel_id=1, source_target_pairs={{0,4},{2,6},{4,0},{6,2},{1,5},{3,7},{5,1},{7,3},{8,12},{10,14},{12... | collective-permute-start | bytes 393224 | tf_op jit(solution)/shard_map/ppermute | solution.py:35
  79.3 2.2 %collective-permute-done.11 = bf16[2,128,256]{2,1,0:T(8,128)(2,1)S(1)} collective-permute-done((bf16[2,128,256]{2,1,0:T(8,128)(2,1)S(1)}, bf16[2,128,256]{2,1,0:T(8,128)(2,1)S(1)}, u32[]{:S(2)}, u32[]{:S(2)}) %collective-permute-start.11) | collective-permute-done | bytes 131104 | tf_op jit(solution)/shard_map/ppermute | solution.py:35
  81.5 3.1 %collective-permute-done.13 = bf16[2,128,256]{2,1,0:T(8,128)(2,1)S(1)} collective-permute-done((bf16[2,128,256]{2,1,0:T(8,128)(2,1)S(1)}, bf16[2,128,256]{2,1,0:T(8,128)(2,1)S(1)}, u32[]{:S(2)}, u32[]{:S(2)}) %collective-permute-start.13) | collective-permute-done | bytes 131104 | tf_op jit(solution)/shard_map/ppermute | solution.py:35
  84.7 2.2 %attend.1 = (bf16[128,256]{1,0:T(8,128)(2,1)S(1)}, f32[2,256,256]{2,1,0:T(8,128)S(1)}, bf16[2,256,256]{2,1,0:T(8,128)(2,1)S(1)}, f32[2,256,256]{2,1,0:T(8,128)S(1)}, bf16[128,256]{1,0:T(8,128)(2,1)S(1)}) custom-call(bf16[2,128,896]{2,1,0:T(8,128)(2,1)S(1)} %bitcast.40, bf16[2,128,896]{2,1,0:T(8,128)(2,1)S(1)} %collective-permute-done.10.oth_ref, ...), custom_call_target="tpu_custom_call" | custom-call | flops 469762048 | bytes 1835008 | tf_op jit(solution)/shard_map/attend/pallas_call | solution.py:149
  88.3 3.1 %collective-permute-start.15 = (bf16[128,256]{1,0:T(8,128)(2,1)S(1)}, bf16[128,256]{1,0:T(8,128)(2,1)S(1)}, u32[]{:S(2)}, u32[]{:S(2)}) collective-permute-start(bf16[128,256]{1,0:T(8,128)(2,1)S(1)} %get-tuple-element.21), channel_id=1, source_target_pairs={{0,4},{2,6},{4,0},{6,2},{1,5},{3,7},{5,1},{7,3},{8,12},{10,14},{12... | collective-permute-start | bytes 196616 | tf_op jit(solution)/shard_map/ppermute | solution.py:35
  91.4 1.9 %backward.1 = (bf16[4,2,32,896]{3,2,1,0:T(8,128)(2,1)S(1)}, bf16[4,2,32,896]{3,2,1,0:T(8,128)(2,1)S(1)}) custom-call(s32[1]{0:T(128)} %bitcast.22.x_ref, f32[2,128,256]{2,1,0:T(8,128)S(1)} %fusion.1.heads_ref, f32[2,256,256]{2,1,0:T(8,128)S(1)} %get-tuple-element.22.key_ref, bf16[2,256,256]{2,1,0:T(8,128)(2,1)S(1)} %get-tuple-element.23.val_ref, ...), custom_call_target="tpu_custom_call" | custom-call | flops 469762048 | bytes 1835008 | tf_op jit(solution)/shard_map/backward/pallas_call | solution.py:192
  98.7 4.2 %all-to-all-start.2 = ((bf16[32,8,512]{2,1,0:T(8,128)(2,1)}), bf16[32,8,512]{2,1,0:T(8,128)(2,1)S(1)}, u32[]{:S(2)}, u32[]{:S(2)}) async-start(bf16[32,8,512]{2,1,0:T(8,128)(2,1)} %output.3), calls=%async_computation.2 | async-start | bytes 524288 | tf_op jit(solution)/shard_map/all_to_all | solution.py:455
  103.1 1.6 %collective-permute-start.20 = (bf16[64,896]{1,0:T(8,128)(2,1)S(1)}, bf16[64,896]{1,0:T(8,128)(2,1)S(1)}, u32[]{:S(2)}, u32[]{:S(2)}) collective-permute-start(bf16[64,896]{1,0:T(8,128)(2,1)S(1)} %bitcast.54), channel_id=1, source_target_pairs={{0,4},{2,6},{4,0},{6,2},{1,5},{3,7},{5,1},{7,3},{8,12},{10,14},{12... | collective-permute-start | bytes 344072 | tf_op jit(solution)/shard_map/ppermute | solution.py:35
  105.8 2.1 %collective-permute-start.19 = (bf16[64,896]{1,0:T(8,128)(2,1)S(1)}, bf16[64,896]{1,0:T(8,128)(2,1)S(1)}, u32[]{:S(2)}, u32[]{:S(2)}) collective-permute-start(bf16[64,896]{1,0:T(8,128)(2,1)S(1)} %bitcast.52), channel_id=1, source_target_pairs={{0,2},{2,0},{4,6},{6,4},{1,3},{3,1},{5,7},{7,5},{8,10},{10,8},{12,... | collective-permute-start | bytes 344072 | tf_op jit(solution)/shard_map/ppermute | solution.py:35
  107.9 2.8 %collective-permute-done.20.t2 = bf16[64,896]{1,0:T(8,128)(2,1)S(1)} collective-permute-done((bf16[64,896]{1,0:T(8,128)(2,1)S(1)}, bf16[64,896]{1,0:T(8,128)(2,1)S(1)}, u32[]{:S(2)}, u32[]{:S(2)}) %collective-permute-start.20) | collective-permute-done | bytes 114720 | tf_op jit(solution)/shard_map/ppermute | solution.py:35
  112.0 4.2 %all-to-all-done.2.piece_ref = bf16[32,8,512]{2,1,0:T(8,128)(2,1)S(1)} async-done(((bf16[32,8,512]{2,1,0:T(8,128)(2,1)}), bf16[32,8,512]{2,1,0:T(8,128)(2,1)S(1)}, u32[]{:S(2)}, u32[]{:S(2)}) %all-to-all-start.2) | async-done | bytes 262176 | tf_op jit(solution)/shard_map/all_to_all | solution.py:455
  116.3 20.4 %all_to_all.21.in_ref = bf16[32,8,768]{2,1,0:T(8,128)(2,1)S(1)} all-to-all(bf16[32,8,768]{2,1,0:T(8,128)(2,1)S(1)} %scan.1), channel_id=1, replica_groups=mesh['segment_0'=8,'segment_1'=4,'tensor_0'=4,'tensor_1'=2] {'segment_0'..., dimensions={0} | all-to-all | bytes 786432 | tf_op jit(solution)/shard_map/all_to_all | solution.py:458
  (80 shorter events, 29.5 us)
Async XLA Ops:
  4.0 1.9 %collective-permute-start = (bf16[256,896]{1,0:T(8,128)(2,1)S(1)}, bf16[256,896]{1,0:T(8,128)(2,1)S(1)}, u32[]{:S(2)}, u32[]{:S(2)}) collective-permute-start(bf16[256,896]{1,0:T(8,128)(2,1)S(1)} %get-tuple-element.16), channel_id=1, source_target_pairs={{0,1},{1,0},{2,3},{3,2},{4,5},{5,4},{6,7},{7,6},{8,9},{9,8},{10,11... | collective-permute-start | bytes 1376264 | tf_op jit(solution)/shard_map/ppermute | solution.py:35
  6.8 28.5 %all-to-all-start = ((bf16[32,8,896]{2,1,0:T(8,128)(2,1)}), bf16[32,8,896]{2,1,0:T(8,128)(2,1)}, u32[]{:S(2)}, u32[]{:S(2)}) async-start(bf16[32,8,896]{2,1,0:T(8,128)(2,1)} %add_bitcast_fusion), calls=%async_computation | async-start | bytes 917504 | tf_op jit(solution)/shard_map/all_to_all | solution.py:426
  27.2 2.7 %collective-permute-start.1 = (bf16[4,2,128,256]{3,2,1,0:T(8,128)(2,1)S(1)}, bf16[4,2,128,256]{3,2,1,0:T(8,128)(2,1)S(1)}, u32[]{:S(2)}, u32[]{:S(2)}) collective-permute-start(bf16[4,2,128,256]{3,2,1,0:T(8,128)(2,1)S(1)} %project.3), channel_id=1, source_target_pairs={{0,1},{1,0},{2,3},{3,2},{4,5},{5,4},{6,7},{7,6},{8,9},{9,8},{10,11... | collective-permute-start | bytes 1572872 | tf_op jit(solution)/shard_map/ppermute | solution.py:35
  36.3 4.2 %collective-permute-start.4 = (bf16[8,896]{1,0:T(8,128)(2,1)S(1)}, bf16[8,896]{1,0:T(8,128)(2,1)S(1)}, u32[]{:S(2)}, u32[]{:S(2)}) collective-permute-start(bf16[8,896]{1,0:T(8,128)(2,1)S(1)} %reduce_sum.21), channel_id=1, source_target_pairs={{0,6},{2,4},{4,2},{6,0},{1,7},{3,5},{5,3},{7,1},{8,14},{10,12},{12... | collective-permute-start | bytes 43016 | tf_op jit(solution)/shard_map/ppermute | solution.py:35
  37.9 5.2 %collective-permute-start.3 = (bf16[8,896]{1,0:T(8,128)(2,1)S(1)}, bf16[8,896]{1,0:T(8,128)(2,1)S(1)}, u32[]{:S(2)}, u32[]{:S(2)}) collective-permute-start(bf16[8,896]{1,0:T(8,128)(2,1)S(1)} %reduce_sum.21), channel_id=1, source_target_pairs={{0,4},{2,6},{4,0},{6,2},{1,5},{3,7},{5,1},{7,3},{8,12},{10,14},{12... | collective-permute-start | bytes 43016 | tf_op jit(solution)/shard_map/ppermute | solution.py:35
  39.0 4.1 %collective-permute-start.2 = (bf16[8,896]{1,0:T(8,128)(2,1)S(1)}, bf16[8,896]{1,0:T(8,128)(2,1)S(1)}, u32[]{:S(2)}, u32[]{:S(2)}) collective-permute-start(bf16[8,896]{1,0:T(8,128)(2,1)S(1)} %reduce_sum.21), channel_id=1, source_target_pairs={{0,2},{2,0},{4,6},{6,4},{1,3},{3,1},{5,7},{7,5},{8,10},{10,8},{12,... | collective-permute-start | bytes 43016 | tf_op jit(solution)/shard_map/ppermute | solution.py:35
  43.1 1.3 collective-permute-start.5
  45.2 1.2 collective-permute-start.6
  46.4 4.2 %collective-permute-start.9 = (bf16[8,896]{1,0:T(8,128)(2,1)S(1)}, bf16[8,896]{1,0:T(8,128)(2,1)S(1)}, u32[]{:S(2)}, u32[]{:S(2)}) collective-permute-start(bf16[8,896]{1,0:T(8,128)(2,1)S(1)} %add_convert_fusion.2), channel_id=1, source_target_pairs={{0,6},{2,4},{4,2},{6,0},{1,7},{3,5},{5,3},{7,1},{8,14},{10,12},{12... | collective-permute-start | bytes 43016 | tf_op jit(solution)/shard_map/ppermute | solution.py:35
  48.3 5.2 %collective-permute-start.8 = (bf16[8,896]{1,0:T(8,128)(2,1)S(1)}, bf16[8,896]{1,0:T(8,128)(2,1)S(1)}, u32[]{:S(2)}, u32[]{:S(2)}) collective-permute-start(bf16[8,896]{1,0:T(8,128)(2,1)S(1)} %add_convert_fusion.2), channel_id=1, source_target_pairs={{0,4},{2,6},{4,0},{6,2},{1,5},{3,7},{5,1},{7,3},{8,12},{10,14},{12... | collective-permute-start | bytes 43016 | tf_op jit(solution)/shard_map/ppermute | solution.py:35
  50.4 3.7 %collective-permute-start.7 = (bf16[8,896]{1,0:T(8,128)(2,1)S(1)}, bf16[8,896]{1,0:T(8,128)(2,1)S(1)}, u32[]{:S(2)}, u32[]{:S(2)}) collective-permute-start(bf16[8,896]{1,0:T(8,128)(2,1)S(1)} %add_convert_fusion.2), channel_id=1, source_target_pairs={{0,2},{2,0},{4,6},{6,4},{1,3},{3,1},{5,7},{7,5},{8,10},{10,8},{12,... | collective-permute-start | bytes 43016 | tf_op jit(solution)/shard_map/ppermute | solution.py:35
  74.9 9.8 %collective-permute-start.10 = (bf16[2,128,896]{2,1,0:T(8,128)(2,1)S(1)}, bf16[2,128,896]{2,1,0:T(8,128)(2,1)S(1)}, u32[]{:S(2)}, u32[]{:S(2)}) collective-permute-start(bf16[2,128,896]{2,1,0:T(8,128)(2,1)S(1)} %bitcast.39), channel_id=1, source_target_pairs={{0,1},{1,0},{2,3},{3,2},{4,5},{5,4},{6,7},{7,6},{8,9},{9,8},{10,11... | collective-permute-start | bytes 1376264 | tf_op jit(solution)/shard_map/ppermute | solution.py:35
  75.0 6.5 %collective-permute-start.11 = (bf16[2,128,256]{2,1,0:T(8,128)(2,1)S(1)}, bf16[2,128,256]{2,1,0:T(8,128)(2,1)S(1)}, u32[]{:S(2)}, u32[]{:S(2)}) collective-permute-start(bf16[2,128,256]{2,1,0:T(8,128)(2,1)S(1)} %get-tuple-element.28), channel_id=1, source_target_pairs={{0,2},{2,0},{4,6},{6,4},{1,3},{3,1},{5,7},{7,5},{8,10},{10,8},{12,... | collective-permute-start | bytes 393224 | tf_op jit(solution)/shard_map/ppermute | solution.py:35
  76.2 8.4 %collective-permute-start.13 = (bf16[2,128,256]{2,1,0:T(8,128)(2,1)S(1)}, bf16[2,128,256]{2,1,0:T(8,128)(2,1)S(1)}, u32[]{:S(2)}, u32[]{:S(2)}) collective-permute-start(bf16[2,128,256]{2,1,0:T(8,128)(2,1)S(1)} %get-tuple-element.29), channel_id=1, source_target_pairs={{0,6},{2,4},{4,2},{6,0},{1,7},{3,5},{5,3},{7,1},{8,14},{10,12},{12... | collective-permute-start | bytes 393224 | tf_op jit(solution)/shard_map/ppermute | solution.py:35
  77.4 7.2 %collective-permute-start.12 = (bf16[2,128,256]{2,1,0:T(8,128)(2,1)S(1)}, bf16[2,128,256]{2,1,0:T(8,128)(2,1)S(1)}, u32[]{:S(2)}, u32[]{:S(2)}) collective-permute-start(bf16[2,128,256]{2,1,0:T(8,128)(2,1)S(1)} %get-tuple-element.30), channel_id=1, source_target_pairs={{0,4},{2,6},{4,0},{6,2},{1,5},{3,7},{5,1},{7,3},{8,12},{10,14},{12... | collective-permute-start | bytes 393224 | tf_op jit(solution)/shard_map/ppermute | solution.py:35
  87.0 6.4 %collective-permute-start.16 = (bf16[128,256]{1,0:T(8,128)(2,1)S(1)}, bf16[128,256]{1,0:T(8,128)(2,1)S(1)}, u32[]{:S(2)}, u32[]{:S(2)}) collective-permute-start(bf16[128,256]{1,0:T(8,128)(2,1)S(1)} %get-tuple-element.21), channel_id=1, source_target_pairs={{0,6},{2,4},{4,2},{6,0},{1,7},{3,5},{5,3},{7,1},{8,14},{10,12},{12... | collective-permute-start | bytes 196616 | tf_op jit(solution)/shard_map/ppermute | solution.py:35
  88.3 6.3 %collective-permute-start.15 = (bf16[128,256]{1,0:T(8,128)(2,1)S(1)}, bf16[128,256]{1,0:T(8,128)(2,1)S(1)}, u32[]{:S(2)}, u32[]{:S(2)}) collective-permute-start(bf16[128,256]{1,0:T(8,128)(2,1)S(1)} %get-tuple-element.21), channel_id=1, source_target_pairs={{0,4},{2,6},{4,0},{6,2},{1,5},{3,7},{5,1},{7,3},{8,12},{10,14},{12... | collective-permute-start | bytes 196616 | tf_op jit(solution)/shard_map/ppermute | solution.py:35
  91.4 4.3 %collective-permute-start.14 = (bf16[128,256]{1,0:T(8,128)(2,1)S(1)}, bf16[128,256]{1,0:T(8,128)(2,1)S(1)}, u32[]{:S(2)}, u32[]{:S(2)}) collective-permute-start(bf16[128,256]{1,0:T(8,128)(2,1)S(1)} %get-tuple-element.21), channel_id=1, source_target_pairs={{0,2},{2,0},{4,6},{6,4},{1,3},{3,1},{5,7},{7,5},{8,10},{10,8},{12,... | collective-permute-start | bytes 196616 | tf_op jit(solution)/shard_map/ppermute | solution.py:35
  93.3 9.6 %collective-permute-start.18 = (bf16[4,2,32,896]{3,2,1,0:T(8,128)(2,1)S(1)}, bf16[4,2,32,896]{3,2,1,0:T(8,128)(2,1)S(1)}, u32[]{:S(2)}, u32[]{:S(2)}) collective-permute-start(bf16[4,2,32,896]{3,2,1,0:T(8,128)(2,1)S(1)} %get-tuple-element.27), channel_id=1, source_target_pairs={{0,1},{1,0},{2,3},{3,2},{4,5},{5,4},{6,7},{7,6},{8,9},{9,8},{10,11... | collective-permute-start | bytes 1376264 | tf_op jit(solution)/shard_map/ppermute | solution.py:35
  95.7 1.6 %collective-permute-start.17 = (bf16[4,128,256]{2,1,0:T(8,128)(2,1)S(1)}, bf16[4,128,256]{2,1,0:T(8,128)(2,1)S(1)}, u32[]{:S(2)}, u32[]{:S(2)}) collective-permute-start(bf16[4,128,256]{2,1,0:T(8,128)(2,1)S(1)} %pad_maximum_fusion.att_ref), channel_id=1, source_target_pairs={{0,1},{1,0},{2,3},{3,2},{4,5},{5,4},{6,7},{7,6},{8,9},{9,8},{10,11... | collective-permute-start | bytes 786440 | tf_op jit(solution)/shard_map/ppermute | solution.py:35
  98.7 17.5 %all-to-all-start.2 = ((bf16[32,8,512]{2,1,0:T(8,128)(2,1)}), bf16[32,8,512]{2,1,0:T(8,128)(2,1)S(1)}, u32[]{:S(2)}, u32[]{:S(2)}) async-start(bf16[32,8,512]{2,1,0:T(8,128)(2,1)} %output.3), calls=%async_computation.2 | async-start | bytes 524288 | tf_op jit(solution)/shard_map/all_to_all | solution.py:455
  103.1 7.6 %collective-permute-start.20 = (bf16[64,896]{1,0:T(8,128)(2,1)S(1)}, bf16[64,896]{1,0:T(8,128)(2,1)S(1)}, u32[]{:S(2)}, u32[]{:S(2)}) collective-permute-start(bf16[64,896]{1,0:T(8,128)(2,1)S(1)} %bitcast.54), channel_id=1, source_target_pairs={{0,4},{2,6},{4,0},{6,2},{1,5},{3,7},{5,1},{7,3},{8,12},{10,14},{12... | collective-permute-start | bytes 344072 | tf_op jit(solution)/shard_map/ppermute | solution.py:35
  104.7 7.1 %collective-permute-start.21 = (bf16[64,896]{1,0:T(8,128)(2,1)S(1)}, bf16[64,896]{1,0:T(8,128)(2,1)S(1)}, u32[]{:S(2)}, u32[]{:S(2)}) collective-permute-start(bf16[64,896]{1,0:T(8,128)(2,1)S(1)} %bitcast.53), channel_id=1, source_target_pairs={{0,6},{2,4},{4,2},{6,0},{1,7},{3,5},{5,3},{7,1},{8,14},{10,12},{12... | collective-permute-start | bytes 344072 | tf_op jit(solution)/shard_map/ppermute | solution.py:35
  105.8 6.0 %collective-permute-start.19 = (bf16[64,896]{1,0:T(8,128)(2,1)S(1)}, bf16[64,896]{1,0:T(8,128)(2,1)S(1)}, u32[]{:S(2)}, u32[]{:S(2)}) collective-permute-start(bf16[64,896]{1,0:T(8,128)(2,1)S(1)} %bitcast.52), channel_id=1, source_target_pairs={{0,2},{2,0},{4,6},{6,4},{1,3},{3,1},{5,7},{7,5},{8,10},{10,8},{12,... | collective-permute-start | bytes 344072 | tf_op jit(solution)/shard_map/ppermute | solution.py:35
  (14 other events, 276.9 us)
where the time goes:
time: 138 us; the launch traced here: 137 us
  blocking collectives  41 us (30%)
  starting transfers between devices  38.5 us (28%)
  waiting for transfers between devices  30.9 us (22%)
  Pallas kernels  14.6 us (11%)
  local copies, waits for them, and re-layouts  8.12 us (6%)
  other arithmetic  3.4 us (2%)
    ppermute x22, starting transfers between devices, swap(): return lax.ppermute(value, axis, [(i, i ^ k) for i in range(size)])  22.6 us
    ppermute x22, waiting for transfers between devices, swap(): return lax.ppermute(value, axis, [(i, i ^ k) for i in range(size)])  22.4 us
    all_to_all x1, blocking collectives, step(): lax.all_to_all(jnp.broadcast_to(encoding[None], (sections, 8, depth)), SE...  20.6 us
    all_to_all x1, blocking collectives, step(): lax.all_to_all(scan(s_index, x_in, contributions, packed), SEGMENT, 0, 0,...  20.4 us
    all_to_all x1, starting transfers between devices, step(): own = lax.all_to_all(paired, SEGMENT, 0, 0, tiled=True)  11.6 us
    unnamed x28, local copies, waits for them, and re-layouts  8.01 us
    pallas_call x2, Pallas kernels, project(): pl.pallas_call(functools.partial(project_kernel, other_core=other_core),...  5.1 us
    all_to_all x1, waiting for transfers between devices, step(): own = lax.all_to_all(paired, SEGMENT, 0, 0, tiled=True)  4.34 us
  transfers between devices with their start and end apart: 24, of which 15 were waited for; matrix products, arithmetic and copies ran while one was open for 1% of the time, Pallas kernels for 7%

commit v1 on v0

--- a/solution.py
+++ b/solution.py
@@ -62,54 +62,69 @@
     return jnp.concatenate([jnp.where(which == h, rows, 0.0) for h in range(heads)], axis=0)
 
 
-def project_kernel(index_ref, x_ref, wq_ref, grad_ref, wo_ref, out_ref, q_buf, o_buf, sem, *, other_core):
-    copies = []
-    for k in range(4):
-        start = pl.multiple_of((index_ref[0] ^ (2 * k + other_core)) * 256, 256)
-        copies.append(
-            (
-                pltpu.make_async_copy(wq_ref.at[:, pl.ds(start, 256)], q_buf.at[k], sem.at[0, k]),
-                pltpu.make_async_copy(wo_ref.at[pl.ds(start, 256), :], o_buf.at[k], sem.at[1, k]),
-            )
-        )
-        for copy in copies[k]:
-            copy.start()
-    for k in range(4):
-        for copy in copies[k]:
-            copy.wait()
-        out_ref[k, 0] = dot(x_ref[...], q_buf[k]).astype(BF16)
-        out_ref[k, 1] = dot(grad_ref[...], o_buf[k], NT).astype(BF16)
-
-
-def project(index, x_in, w_query, grad, w_out, other_core):
+def project_kernel(index_ref, x_hbm, wq_ref, grad_hbm, wo_ref, send_ref, keep_ref,
+                   x_ref, grad_ref, q_buf, o_buf, acc_ref, out_buf, sem):
+    starts, outs, ins, back = [], [], [], []
+    small = [
+        pltpu.make_async_copy(x_hbm, x_ref, sem.at[12]),
+        pltpu.make_async_copy(grad_hbm, grad_ref, sem.at[13]),
+    ]
+    for part in range(4):
+        rows = slice(part * 256, (part + 1) * 256)
+        ins.append(pltpu.make_async_copy(wq_ref.at[rows, :], q_buf.at[part], sem.at[8 + part]))
+    for k in range(8):
+        start = pl.multiple_of((index_ref[0] ^ (2 * (k % 4) + 1 - k // 4)) * 256, 256)
+        starts.append(start)
+        outs.append(pltpu.make_async_copy(wo_ref.at[pl.ds(start, 256), :], o_buf.at[k], sem.at[k]))
+        out_ref = keep_ref if k // 4 else send_ref
+        back.append(pltpu.make_async_copy(out_buf.at[k], out_ref.at[k % 4], sem.at[14 + k]))
+    for copy in small + ins + outs:
+        copy.start()
+    small[0].wait()
+    for part in range(4):
+        ins[part].wait()
+        rows = x_ref[:, part * 256 : (part + 1) * 256]
+        for column in range(4):
+            lanes = slice(column * 512, (column + 1) * 512)
+            added = dot(rows, q_buf[part, :, lanes])
+            acc_ref[:, lanes] = added if part == 0 else acc_ref[:, lanes] + added
+    small[1].wait()
+    for k in range(8):
+        out_buf[k, 0] = acc_ref[:, pl.ds(starts[k], 256)].astype(BF16)
+        outs[k].wait()
+        out_buf[k, 1] = dot(grad_ref[...], o_buf[k], NT).astype(BF16)
+        back[k].start()
+    for copy in back:
+        copy.wait()
+
+
+def project(index, x_in, w_query, grad, w_out):
     tokens, depth = x_in.shape
     shape = (4, 2, tokens, 256)
-    anywhere = pl.BlockSpec(memory_space=pltpu.HBM)
-    return pl.pallas_call(
-        functools.partial(project_kernel, other_core=other_core),
-        out_shape=jax.ShapeDtypeStruct(shape, BF16),
-        in_specs=[
-            pl.BlockSpec(memory_space=pltpu.SMEM),
-            whole((tokens, depth)),
-            anywhere,
-            whole((tokens, depth)),
-            anywhere,
-        ],
-        out_specs=whole(shape),
+    far = pl.BlockSpec(memory_space=pltpu.HBM)
+    return pl.pallas_call(
+        project_kernel,
+        out_shape=[jax.ShapeDtypeStruct(shape, BF16)] * 2,
+        in_specs=[pl.BlockSpec(memory_space=pltpu.SMEM)] + [far] * 4,
+        out_specs=[far] * 2,
         scratch_shapes=[
-            pltpu.VMEM((4, depth, 256), BF16),
-            pltpu.VMEM((4, 256, depth), BF16),
-            pltpu.SemaphoreType.DMA((2, 4)),
+            pltpu.VMEM(x_in.shape, BF16),
+            pltpu.VMEM(grad.shape, BF16),
+            pltpu.VMEM((4, 256, w_query.shape[1]), BF16),
+            pltpu.VMEM((8, 256, depth), BF16),
+            pltpu.VMEM((tokens, w_query.shape[1]), F32),
+            pltpu.VMEM((8, 2, tokens, 256), BF16),
+            pltpu.SemaphoreType.DMA((22,)),
         ],
         cost_estimate=pl.CostEstimate(
-            flops=16 * tokens * depth * 256, bytes_accessed=16 * depth * 256, transcendentals=0
-        ),
-        compiler_params=PARAMS,
+            flops=32 * tokens * depth * 256, bytes_accessed=32 * depth * 256, transcendentals=0
+        ),
+        compiler_params=pltpu.CompilerParams(vmem_limit_bytes=60 << 20),
         name="project",
     )(index, x_in, w_query, grad, w_out)
 
 
-def attend_kernel(own_ref, oth_ref, wk_ref, wv_ref, heads_ref, att_ref,
+def attend_kernel(own_ref, oth_ref, order_ref, wk_ref, wv_ref, heads_ref, att_ref,
                   key_ref, val_ref, weight_ref, qhat_ref):
     wk = wk_ref[...]
     wv = wv_ref[...]
@@ -117,7 +132,9 @@
     query = query * lax.rsqrt(head_mean(query * query) + EPSILON)
     qhat_ref[...] = query.astype(BF16)
     for span in range(2):
-        enc = jnp.concatenate([own_ref[span], oth_ref[span]], axis=0)
+        places = slice(span * 256, (span + 1) * 256)
+        enc = dot(order_ref[:256, places], own_ref[...], TN)
+        enc = (enc + dot(order_ref[256:, places], oth_ref[...], TN)).astype(BF16)
         key = dot(enc, wk)
         value = dot(enc, wv).astype(BF16)
         key_ref[span] = key
@@ -141,7 +158,7 @@
     return pl.BlockSpec(shape, lambda: (0,) * len(shape))
 
 
-def attend(own, oth, w_key, w_value, heads):
+def attend(own, oth, places, w_key, w_value, heads):
     depth = w_key.shape[0]
     piece = whole((2, 128, 256))
     shapes = [((128, 256), BF16), ((2, 256, 256), F32), ((2, 256, 256), BF16),
@@ -149,14 +166,14 @@
     return pl.pallas_call(
         attend_kernel,
         out_shape=[jax.ShapeDtypeStruct(*s) for s in shapes],
-        in_specs=[whole((2, 128, depth))] * 2 + [whole((depth, 256))] * 2 + [piece],
+        in_specs=[whole((256, depth))] * 2 + [whole((512, 512))] + [whole((depth, 256))] * 2 + [piece],
         out_specs=[whole(s[0]) for s in shapes],
         cost_estimate=pl.CostEstimate(
             flops=4 * 512 * depth * 256, bytes_accessed=4 * 512 * depth, transcendentals=131072
         ),
         compiler_params=PARAMS,
         name="attend",
-    )(own, oth, w_key, w_value, heads)
+    )(own, oth, places, w_key, w_value, heads)
 
 
 def backward_kernel(x_ref, heads_ref, key_ref, val_ref, weight_ref, qhat_ref, wk_ref, wv_ref,
@@ -253,36 +270,180 @@
     )(index, att, w_out, *([base] if second else []))
 
 
-def lookup_kernel(index_ref, ids_ref, table_ref, own_ref, oth_ref):
-    core = index_ref[0]
-    ids = ids_ref[...] - index_ref[1]
+def one_hot(condition):
+    return jnp.where(condition, 1.0, 0.0)
+
+
+def lookup_kernel(index_ref, ids_ref, table_ref, out_ref, sel_ref, idx_ref, over_ref, table_buf, wide_ref, sem):
+    copy = pltpu.make_async_copy(table_ref, table_buf, sem)
+    copy.start()
+    core, first_row, section, x = (index_ref[i] for i in range(4))
+    ids = ids_ref[...]
     depth, count = table_ref.shape[0], ids.shape[1]
-    hot = jnp.where(lax.broadcasted_iota(jnp.int32, (depth, count), 0) == ids, 1.0, 0.0).astype(BF16)
-    source = lax.broadcasted_iota(jnp.int32, (count, count // 2), 0)
-    place = lax.broadcasted_iota(jnp.int32, (count, count // 2), 1)
-    token = ((place >> 7) << 8) + (((place >> 1) & 15) << 4) + (((place >> 5) & 3) << 2) + (place & 1)
-    for out_ref, which in ((oth_ref, 1 - core), (own_ref, core)):
-        pick = jnp.where(source == token + 2 * which, 1.0, 0.0).astype(BF16)
-        out_ref[...] = dot(dot(hot, pick).astype(BF16), table_ref[...], TN).astype(BF16)
+    left = lax.broadcasted_iota(jnp.int32, (count, count), 0)
+    right = lax.broadcasted_iota(jnp.int32, (count, count), 1)
+
+    def columns(row):
+        part = jnp.transpose(jnp.broadcast_to(row, (128, count)))
+        return jnp.concatenate([part] * (count // 128), axis=1)
+
+    ids_row = ids.astype(F32)
+    ids_col = columns(ids_row)
+    less = (ids_col < ids_row) | ((ids_col == ids_row) & (left < right))
+    rank_row = jnp.sum(one_hot(less), axis=0, keepdims=True)
+    rank = rank_row.astype(jnp.int32)
+    rank_col = columns(rank_row)[:, :128].astype(jnp.int32)
+
+    shard = lax.broadcasted_iota(jnp.int32, (256, count), 0)
+    most = jnp.max(jnp.sum(one_hot((ids >> 8) == shard), axis=1, keepdims=True), axis=0, keepdims=True)
+    over = most > 64.0
+    over_ref[...] = jnp.broadcast_to(jnp.where(over, 1, 0), over_ref.shape)
+
+    hot = one_hot(lax.broadcasted_iota(jnp.int32, (depth, count), 0) == ids - first_row).astype(BF16)
+    lane = lax.broadcasted_iota(jnp.int32, (count, 128), 1)
+    block = 2 * (lane & 31) + jnp.where(lane < 32, core, 1 - core)
+    pick = one_hot((rank_col & 63) == block).astype(BF16)
+    picked = dot(hot, pick).astype(BF16)
+
+    turn = lax.broadcasted_iota(jnp.int32, (16, count), 0)
+    slot = (turn & 7) * 64 + 2 * section + jnp.where(turn < 8, core, 1 - core)
+    owner = jnp.sum(jnp.where(rank == slot, ids_row, 0.0), axis=1, keepdims=True).astype(jnp.int32)
+    source = lax.broadcasted_iota(jnp.int32, (16, 128), 1)
+    here = (source == (owner >> 11)) & (((owner >> 8) & 7) == 2 * x + core) & (most <= 64.0)
+    sel_ref[...] = one_hot(here).astype(BF16)
+    block = rank & 63
+    idx_ref[...] = ((block & 1) ^ core) * 256 + (block >> 1) * 8 + (rank >> 6)
+
+    copy.wait()
+    rows = dot(picked, table_buf[...], TN)
+    wide_ref[...] = jnp.zeros_like(wide_ref)
+    for chunk in range(7):
+        lanes = slice(chunk * 128, (chunk + 1) * 128)
+        wide_ref[:, chunk, :] = rows[:32, lanes]
+        wide_ref[:, 8 + chunk, :] = rows[32:64, lanes]
+    out_ref[...] = wide_ref[...].astype(BF16)
 
 
 def lookup(index, ids, table):
-    shape = (ids.shape[1] // 2, table.shape[1])
+    shapes = [((32, 16, 128), BF16), ((16, 128), BF16), (ids.shape, jnp.int32), ((8, 128), jnp.int32)]
     return pl.pallas_call(
         lookup_kernel,
-        out_shape=[jax.ShapeDtypeStruct(shape, BF16)] * 2,
-        in_specs=[pl.BlockSpec(memory_space=pltpu.SMEM), whole(ids.shape), whole(table.shape)],
-        out_specs=[whole(shape)] * 2,
+        out_shape=[jax.ShapeDtypeStruct(*s) for s in shapes],
+        in_specs=[
+            pl.BlockSpec(memory_space=pltpu.SMEM),
+            whole(ids.shape),
+            pl.BlockSpec(memory_space=pltpu.HBM),
+        ],
+        out_specs=[whole(s[0]) for s in shapes],
+        scratch_shapes=[
+            pltpu.VMEM(table.shape, BF16),
+            pltpu.VMEM((32, 16, 128), F32),
+            pltpu.SemaphoreType.DMA,
+        ],
         cost_estimate=pl.CostEstimate(
-            flops=4 * 256 * 256 * 896, bytes_accessed=4 * 512 * 896, transcendentals=0
+            flops=2 * 128 * 256 * 896, bytes_accessed=2 * 256 * 896, transcendentals=0
         ),
         compiler_params=PARAMS,
         name="lookup",
     )(index, ids, table)
 
 
-def encode_kernel(own_ref, oth_ref, gate_ref, up_ref, down_ref, keep_ref, send_ref):
-    rows = jnp.concatenate([own_ref[...], oth_ref[...]], axis=0)
+def place_kernel(sel_ref, piece_ref, out_ref, wide_ref):
+    wide_ref[...] = piece_ref[...].astype(F32)
+    sel = sel_ref[:, :32]
+    for chunk in range(7):
+        lanes = slice(chunk * 128, (chunk + 1) * 128)
+        for half in range(2):
+            slots = slice(half * 8, half * 8 + 8)
+            rows = dot(sel[slots], wide_ref[:, half * 8 + chunk, :].astype(BF16))
+            out_ref[slots, lanes] = rows.astype(BF16)
+
+
+def place(sel, pieces):
+    shape = (sel.shape[0], 896)
+    return pl.pallas_call(
+        place_kernel,
+        out_shape=jax.ShapeDtypeStruct(shape, BF16),
+        in_specs=[whole(sel.shape), whole(pieces.shape)],
+        out_specs=whole(shape),
+        scratch_shapes=[pltpu.VMEM(pieces.shape, F32)],
+        cost_estimate=pl.CostEstimate(flops=917504, bytes_accessed=172032, transcendentals=0),
+        compiler_params=PARAMS,
+        name="place",
+    )(sel, pieces)
+
+
+def order_kernel(index_ref, idx_ref, out_ref):
+    core = index_ref[0]
+    count = idx_ref.shape[1]
+    source = lax.broadcasted_iota(jnp.int32, (count, count), 0)
+    place = lax.broadcasted_iota(jnp.int32, (count, count), 1)
+    kind = ((place >> 7) & 1) ^ core
+    token = ((place >> 8) << 8) + (((place >> 1) & 15) << 4) + (((place >> 5) & 3) << 2)
+    token = token + 2 * kind + (place & 1)
+    found = one_hot(source == idx_ref[...]).astype(BF16)
+    out_ref[...] = dot(found, one_hot(source == token).astype(BF16)).astype(BF16)
+
+
+def order(index, idx):
+    shape = (idx.shape[1], idx.shape[1])
+    return pl.pallas_call(
+        order_kernel,
+        out_shape=jax.ShapeDtypeStruct(shape, BF16),
+        in_specs=[pl.BlockSpec(memory_space=pltpu.SMEM), whole(idx.shape)],
+        out_specs=whole(shape),
+        cost_estimate=pl.CostEstimate(flops=2 * 512**3, bytes_accessed=526336, transcendentals=0),
+        compiler_params=PARAMS,
+        name="order",
+    )(index, idx)
+
+
+def dense_lookup(core, first_row, ids, table):
+    count = ids.shape[0]
+    tokens = jnp.arange(count, dtype=jnp.int32)
+    less = (ids[:, None] < ids[None, :]) | (
+        (ids[:, None] == ids[None, :]) & (tokens[:, None] < tokens[None, :])
+    )
+    rank = jnp.sum(less.astype(jnp.int32), axis=0)
+    shape = (32, 8)
+    block = 2 * lax.broadcasted_iota(jnp.int32, shape, 0)
+    turn = 64 * lax.broadcasted_iota(jnp.int32, shape, 1)
+    rows = jnp.arange(table.shape[0], dtype=jnp.int32)
+
+    def rows_of(which):
+        wanted = (block + turn + which).reshape(-1, 1)
+        chosen = jnp.sum(jnp.where(wanted == rank[None, :], ids[None, :], 0), axis=1)
+        hot = (chosen[:, None] - first_row == rows[None, :]).astype(BF16)
+        return dot(hot, table).astype(BF16)
+
+    rows = jnp.concatenate(
+        [rows_of(which).reshape(*shape, table.shape[1]) for which in (core, 1 - core)], axis=1
+    )
+    arrived = lax.all_to_all(rows, SEGMENT, 0, 0, tiled=True)
+    return gathered_sum(jnp.sum(arrived.astype(F32), axis=0).astype(BF16)).astype(BF16)
+
+
+def settle_kernel(own_ref, p0, p1, p2, p3, out_ref):
+    resid = own_ref[...].astype(F32) + sum(p[...].astype(F32) for p in (p0, p1, p2, p3))
+    scale = lax.rsqrt(jnp.mean(resid * resid, axis=-1, keepdims=True) + EPSILON)
+    out_ref[...] = jnp.broadcast_to((resid * scale).astype(BF16)[None], out_ref.shape)
+
+
+def settle(own, parts, copies):
+    shape = (copies, *own.shape)
+    return pl.pallas_call(
+        settle_kernel,
+        out_shape=jax.ShapeDtypeStruct(shape, BF16),
+        in_specs=[whole(own.shape)] * 5,
+        out_specs=whole(shape),
+        cost_estimate=pl.CostEstimate(flops=57344, bytes_accessed=458752, transcendentals=8),
+        compiler_params=PARAMS,
+        name="settle",
+    )(own, *parts)
+
+
+def encode_kernel(rows_ref, gate_ref, up_ref, down_ref, keep_ref, send_ref):
+    rows = rows_ref[...]
     gate = dot(rows, gate_ref[...], NT)
     hidden = (gate / (1.0 + jnp.exp(-gate)) * dot(rows, up_ref[...], NT)).astype(BF16)
     partial = dot(hidden, down_ref[...])
@@ -290,13 +451,14 @@
     send_ref[...] = partial[8:].astype(BF16)
 
 
-def encode(own, oth, enc_gate, enc_up, enc_down):
-    operands = (own, oth, enc_gate.T, enc_up.T, enc_down)
+def encode(rows, enc_gate, enc_up, enc_down):
+    operands = (rows, enc_gate.T, enc_up.T, enc_down)
+    shape = (8, rows.shape[1])
     return pl.pallas_call(
         encode_kernel,
-        out_shape=[jax.ShapeDtypeStruct(own.shape, F32), jax.ShapeDtypeStruct(own.shape, BF16)],
+        out_shape=[jax.ShapeDtypeStruct(shape, F32), jax.ShapeDtypeStruct(shape, BF16)],
         in_specs=[whole(o.shape) for o in operands],
-        out_specs=[whole(own.shape)] * 2,
+        out_specs=[whole(shape)] * 2,
         cost_estimate=pl.CostEstimate(
             flops=6 * 16 * 896 * 448, bytes_accessed=6 * 896 * 448, transcendentals=8192
         ),
@@ -390,10 +552,9 @@
     )(arrived)
 
 
-def gathered_sum(value, keep=None):
+def gathered_sum(value, extra=0.0):
     parts = [swap(value, X, k) for k in (1, 2, 3)]
-    total = value.astype(F32) if keep is None else keep
-    return total + sum(p.astype(F32) for p in parts)
+    return value.astype(F32) + sum(p.astype(F32) for p in parts) + extra
 
 
 def step(
@@ -419,34 +580,38 @@
     vocab_rows, depth = embed_table.shape
     first_row = (section * lax.axis_size(TENSOR) + tensor) * vocab_rows
 
-    found, passed = lookup(jnp.stack([core.astype(jnp.int32), first_row]), neighbour_ids[None], embed_table)
-    paired = (found + swap(passed, C, 1)).reshape(sections, 8, depth)
+    core = core.astype(jnp.int32)
+    index = jnp.stack([core, first_row, section, x_index[0]])
+    found, sel, idx, over = lookup(index, neighbour_ids[None], embed_table)
     w_query, w_key, w_value, w_out = query_weight[0], key_weight[0], value_weight[0], out_weight[0]
     grad_local = state_grad[0]
-    own = lax.all_to_all(paired, SEGMENT, 0, 0, tiled=True)
-    sent = project(t_index, x_in, w_query, grad_local, w_out, 1)
+    own = lax.all_to_all(found, SEGMENT, 0, 0, tiled=True)
+    sent, kept = project(t_index, x_in, w_query, grad_local, w_out)
+    dense = lax.cond(
+        over[0, 0] > 0,
+        lambda ids, table: dense_lookup(core, first_row, ids, table),
+        lambda ids, table: jnp.zeros((16, depth), BF16),
+        neighbour_ids,
+        embed_table,
+    )
     sent = swap(sent, C, 1)
-    kept = project(t_index, x_in, w_query, grad_local, w_out, 0)
     both = (kept.astype(F32) + sent.astype(F32)).astype(BF16)
-    own, both = lax.optimization_barrier((own, both))
     pieces = [both[0]] + [swap(both[k], X, k) for k in (1, 2, 3)]
     heads = sum(p.astype(F32) for p in pieces)
-
-    own = jnp.sum(own.astype(F32), axis=0).astype(BF16)
-    own = gathered_sum(own).astype(BF16)
-    keep, send = encode(own, swap(own, C, 1), enc_gate, enc_up, enc_down)
+    idx, heads = lax.optimization_barrier((idx, heads))
+    places = order(core[None], idx)
+
+    rows = gathered_sum(place(sel, own), dense.astype(F32)).astype(BF16)
+    rows = rows + swap(jnp.concatenate([rows[8:], rows[:8]], axis=0), C, 1)
+    own = rows[:8]
+    keep, send = encode(rows, enc_gate, enc_up, enc_down)
     partial = (keep + swap(send, C, 1).astype(F32)).astype(BF16)
-    resid = own.astype(F32) + gathered_sum(partial)
-    encoding = (
-        resid * lax.rsqrt(jnp.mean(resid * resid, axis=-1, keepdims=True) + EPSILON)
-    ).astype(BF16)
-    enc_own = lax.all_to_all(
-        jnp.broadcast_to(encoding[None], (sections, 8, depth)), SEGMENT, 0, 0, tiled=True
-    )
-    enc_own = enc_own.reshape(2, 128, depth)
+    copies = settle(own, [partial] + [swap(partial, X, k) for k in (1, 2, 3)], sections)
+    enc_own = lax.all_to_all(copies, SEGMENT, 0, 0, tiled=True)
+    enc_own = enc_own.reshape(256, depth)
     enc_oth = swap(enc_own, C, 1)
 
-    att, *saved = attend(enc_own, enc_oth, w_key, w_value, heads)
+    att, *saved = attend(enc_own, enc_oth, places, w_key, w_value, heads)
     atts = jnp.stack([att] + [swap(att, X, k) for k in (1, 2, 3)])
     keep, send = backward(x_index, heads, saved, w_key, w_value)
     atts_other = swap(atts, C, 1)

time: 138 us -> 129 us (0.935)
  starting transfers between devices: 38.5 us -> 31 us
  local copies, waits for them, and re-layouts: 8.12 us -> 0.7 us
  Pallas kernels: 14.6 us -> 19.2 us
  other arithmetic: 3.4 us -> 1.59 us
  waiting for transfers between devices: 30.9 us -> 32.5 us
    unnamed x28 -> x14, local copies, waits for them, and re-layouts: 8.01 us -> 0.04 us
    all_to_all x1, starting transfers between devices: 11.6 us -> 4.06 us  [step(): enc_own = lax.all_to_all(copies, SEGMENT, 0, 0, tiled=True)]
    pallas_call x4 -> x6, Pallas kernels: 7.43 us -> 11.5 us  [the longest x1 6.95 us: project(): pl.pallas_call(project_kernel, out_shape=[jax.ShapeDtypeStruct(shape, BF1...]
    ppermute x22 -> x21, waiting for transfers between devices: 22.4 us -> 23 us  [swap(): return lax.ppermute(value, axis, [(i, i ^ k) for i in range(size)])]
    ppermute x22 -> x21, starting transfers between devices: 22.6 us -> 22.4 us  [swap(): return lax.ppermute(value, axis, [(i, i ^ k) for i in range(size)])]
  transfers between devices with their start and end apart: 24 -> 23, of which waited for: 15 -> 16; matrix products, arithmetic and copies ran while one was open for 1% -> 1% of each run, Pallas kernels for 7% -> 9%
where the time goes in v1:
time: 129 us
  blocking collectives  42.3 us (33%)
  waiting for transfers between devices  32.5 us (25%)
  starting transfers between devices  31 us (24%)
  Pallas kernels  19.2 us (15%)
  between operations  1.63 us (1%)
  other arithmetic  1.59 us (1%)
    ppermute x21, waiting for transfers between devices, swap(): return lax.ppermute(value, axis, [(i, i ^ k) for i in range(size)])  23 us
    ppermute x21, starting transfers between devices, swap(): return lax.ppermute(value, axis, [(i, i ^ k) for i in range(size)])  22.4 us
    all_to_all x1, blocking collectives, step(): own = lax.all_to_all(found, SEGMENT, 0, 0, tiled=True)  21.9 us
    all_to_all x1, blocking collectives, step(): lax.all_to_all(scan(s_index, x_in, contributions, packed), SEGMENT, 0, 0,...  20.4 us
    pallas_call x1, Pallas kernels, project(): pl.pallas_call(project_kernel, out_shape=[jax.ShapeDtypeStruct(shape, BF1...  6.95 us
    all_to_all x1, waiting for transfers between devices, step(): enc_own = lax.all_to_all(copies, SEGMENT, 0, 0, tiled=True)  5.29 us
    all_to_all x1, starting transfers between devices, step(): contributions = lax.all_to_all(contribution, SEGMENT, 0, 0, tiled=True)  4.55 us
    all_to_all x1, waiting for transfers between devices, step(): contributions = lax.all_to_all(contribution, SEGMENT, 0, 0, tiled=True)  4.16 us
  transfers between devices with their start and end apart: 23, of which 16 were waited for; matrix products, arithmetic and copies ran while one was open for 1% of the time, Pallas kernels for 9%

profile of v1, /device:TPU:2, one launch (start us, length us, event | category | flops | bytes accessed | tf_op | source)
XLA Modules:
  0.0 128.8 jit_solution(569985860738199403)
XLA Ops:
  0.7 2.0 %lookup.1 = (bf16[32,16,128]{2,1,0:T(8,128)(2,1)S(1)}, bf16[16,128]{1,0:T(8,128)(2,1)S(1)}, s32[1,512]{1,0:T(1,128)S(1)}, s32[8,128]{1,0:T(8,128)S(1)}) custom-call(s32[4]{0:T(128)S(1)} %pad_add_fusion.index_ref, s32[1,512]{1,0:T(1,128)} %bitcast.61, bf16[256,896]{1,0:T(8,128)(2,1)} %table_ref.1), custom_call_target="tpu_custom_call" | custom-call | flops 58720256 | bytes 458752 | tf_op jit(solution)/shard_map/lookup/pallas_call | solution.py:329
  4.1 21.9 %all_to_all.25.piece_ref = bf16[32,16,128]{2,1,0:T(8,128)(2,1)S(1)} all-to-all(bf16[32,16,128]{2,1,0:T(8,128)(2,1)S(1)} %get-tuple-element.36), channel_id=1, replica_groups=mesh['segment_0'=8,'segment_1'=4,'tensor_0'=4,'tensor_1'=2] {'segment_0'..., dimensions={0} | all-to-all | bytes 262144 | tf_op jit(solution)/shard_map/all_to_all | solution.py:588
  26.3 1.5 %collective-permute-start.5 = (bf16[16,896]{1,0:T(8,128)(2,1)S(1)}, bf16[16,896]{1,0:T(8,128)(2,1)S(1)}, u32[]{:S(2)}, u32[]{:S(2)}) collective-permute-start(bf16[16,896]{1,0:T(8,128)(2,1)S(1)} %place.1), channel_id=1, source_target_pairs={{0,6},{2,4},{4,2},{6,0},{1,7},{3,5},{5,3},{7,1},{8,14},{10,12},{12... | collective-permute-start | bytes 86024 | tf_op jit(solution)/shard_map/ppermute | solution.py:35
  29.0 1.5 %collective-permute-start.3 = (bf16[16,896]{1,0:T(8,128)(2,1)S(1)}, bf16[16,896]{1,0:T(8,128)(2,1)S(1)}, u32[]{:S(2)}, u32[]{:S(2)}) collective-permute-start(bf16[16,896]{1,0:T(8,128)(2,1)S(1)} %place.1), channel_id=1, source_target_pairs={{0,2},{2,0},{4,6},{6,4},{1,3},{3,1},{5,7},{7,5},{8,10},{10,8},{12,... | collective-permute-start | bytes 86024 | tf_op jit(solution)/shard_map/ppermute | solution.py:35
  30.6 2.7 %collective-permute-done.4 = bf16[16,896]{1,0:T(8,128)(2,1)S(1)} collective-permute-done((bf16[16,896]{1,0:T(8,128)(2,1)S(1)}, bf16[16,896]{1,0:T(8,128)(2,1)S(1)}, u32[]{:S(2)}, u32[]{:S(2)}) %collective-permute-start.4) | collective-permute-done | bytes 28704 | tf_op jit(solution)/shard_map/ppermute | solution.py:35
  36.6 1.8 %collective-permute-start.10 = (bf16[8,896]{1,0:T(8,128)(2,1)S(1)}, bf16[8,896]{1,0:T(8,128)(2,1)S(1)}, u32[]{:S(2)}, u32[]{:S(2)}) collective-permute-start(bf16[8,896]{1,0:T(8,128)(2,1)S(1)} %add_convert_fusion.4.p0), channel_id=1, source_target_pairs={{0,6},{2,4},{4,2},{6,0},{1,7},{3,5},{5,3},{7,1},{8,14},{10,12},{12... | collective-permute-start | bytes 43016 | tf_op jit(solution)/shard_map/ppermute | solution.py:35
  38.5 2.1 %collective-permute-start.9 = (bf16[8,896]{1,0:T(8,128)(2,1)S(1)}, bf16[8,896]{1,0:T(8,128)(2,1)S(1)}, u32[]{:S(2)}, u32[]{:S(2)}) collective-permute-start(bf16[8,896]{1,0:T(8,128)(2,1)S(1)} %add_convert_fusion.4.p0), channel_id=1, source_target_pairs={{0,4},{2,6},{4,0},{6,2},{1,5},{3,7},{5,1},{7,3},{8,12},{10,14},{12... | collective-permute-start | bytes 43016 | tf_op jit(solution)/shard_map/ppermute | solution.py:35
  40.8 2.9 %collective-permute-done.9.p2 = bf16[8,896]{1,0:T(8,128)(2,1)S(1)} collective-permute-done((bf16[8,896]{1,0:T(8,128)(2,1)S(1)}, bf16[8,896]{1,0:T(8,128)(2,1)S(1)}, u32[]{:S(2)}, u32[]{:S(2)}) %collective-permute-start.9) | collective-permute-done | bytes 14368 | tf_op jit(solution)/shard_map/ppermute | solution.py:35
  45.2 4.1 %all-to-all-start.2 = ((bf16[32,8,896]{2,1,0:T(8,128)(2,1)}), bf16[32,8,896]{2,1,0:T(8,128)(2,1)S(1)}, u32[]{:S(2)}, u32[]{:S(2)}) async-start(bf16[32,8,896]{2,1,0:T(8,128)(2,1)} %settle.1), calls=%async_computation.2 | async-start | bytes 917504 | tf_op jit(solution)/shard_map/all_to_all | solution.py:610
  49.3 7.0 %project.1 = (bf16[4,2,128,256]{3,2,1,0:T(8,128)(2,1)}, bf16[4,2,128,256]{3,2,1,0:T(8,128)(2,1)}) custom-call(s32[1]{0:T(128)} %bitcast.3.index_ref, bf16[128,1024]{1,0:T(8,128)(2,1)} %x_ref.1, bf16[1024,2048]{1,0:T(8,128)(2,1)} %bitcast.53, bf16[128,1024]{1,0:T(8,128)(2,1)} %bitcast.54, bf16[2048,1024]{1,0:T(8,128)(2,1)} %bitcast.40), custom_call_target="tpu_custom_call" | custom-call | flops 1073741824 | bytes 8388608 | tf_op jit(solution)/shard_map/project/pallas_call | solution.py:105
  56.4 2.1 %collective-permute-done.12 = bf16[4,2,128,256]{3,2,1,0:T(8,128)(2,1)S(1)} collective-permute-done((bf16[4,2,128,256]{3,2,1,0:T(8,128)(2,1)}, bf16[4,2,128,256]{3,2,1,0:T(8,128)(2,1)S(1)}, u32[]{:S(2)}, u32[]{:S(2)}) %collective-permute-start.12) | collective-permute-done | bytes 524320 | tf_op jit(solution)/shard_map/ppermute | solution.py:35
  59.7 5.3 %all-to-all-done.2 = bf16[32,8,896]{2,1,0:T(8,128)(2,1)S(1)} async-done(((bf16[32,8,896]{2,1,0:T(8,128)(2,1)}), bf16[32,8,896]{2,1,0:T(8,128)(2,1)S(1)}, u32[]{:S(2)}, u32[]{:S(2)}) %all-to-all-start.2) | async-done | bytes 458784 | tf_op jit(solution)/shard_map/all_to_all | solution.py:610
  67.5 1.7 %collective-permute-start.14 = (bf16[2,128,256]{2,1,0:T(8,128)(2,1)S(1)}, bf16[2,128,256]{2,1,0:T(8,128)(2,1)S(1)}, u32[]{:S(2)}, u32[]{:S(2)}) collective-permute-start(bf16[2,128,256]{2,1,0:T(8,128)(2,1)S(1)} %get-tuple-element.60), channel_id=1, source_target_pairs={{0,4},{2,6},{4,0},{6,2},{1,5},{3,7},{5,1},{7,3},{8,12},{10,14},{12... | collective-permute-start | bytes 393224 | tf_op jit(solution)/shard_map/ppermute | solution.py:35
  69.2 2.0 %collective-permute-done.13 = bf16[2,128,256]{2,1,0:T(8,128)(2,1)S(1)} collective-permute-done((bf16[2,128,256]{2,1,0:T(8,128)(2,1)S(1)}, bf16[2,128,256]{2,1,0:T(8,128)(2,1)S(1)}, u32[]{:S(2)}, u32[]{:S(2)}) %collective-permute-start.13) | collective-permute-done | bytes 131104 | tf_op jit(solution)/shard_map/ppermute | solution.py:35
  71.2 3.5 %collective-permute-done.15 = bf16[2,128,256]{2,1,0:T(8,128)(2,1)S(1)} collective-permute-done((bf16[2,128,256]{2,1,0:T(8,128)(2,1)S(1)}, bf16[2,128,256]{2,1,0:T(8,128)(2,1)S(1)}, u32[]{:S(2)}, u32[]{:S(2)}) %collective-permute-start.15) | collective-permute-done | bytes 131104 | tf_op jit(solution)/shard_map/ppermute | solution.py:35
  75.3 2.8 %attend.1 = (bf16[128,256]{1,0:T(8,128)(2,1)S(1)}, f32[2,256,256]{2,1,0:T(8,128)S(1)}, bf16[2,256,256]{2,1,0:T(8,128)(2,1)S(1)}, f32[2,256,256]{2,1,0:T(8,128)S(1)}, bf16[128,256]{1,0:T(8,128)(2,1)S(1)}) custom-call(bf16[256,896]{1,0:T(8,128)(2,1)S(1)} %bitcast.44, bf16[256,896]{1,0:T(8,128)(2,1)S(1)} %collective-permute-done.11.oth_ref, ...), custom_call_target="tpu_custom_call" | custom-call | flops 469762048 | bytes 1835008 | tf_op jit(solution)/shard_map/attend/pallas_call | solution.py:166
  79.4 2.9 %collective-permute-start.17 = (bf16[128,256]{1,0:T(8,128)(2,1)S(1)}, bf16[128,256]{1,0:T(8,128)(2,1)S(1)}, u32[]{:S(2)}, u32[]{:S(2)}) collective-permute-start(bf16[128,256]{1,0:T(8,128)(2,1)S(1)} %get-tuple-element.45), channel_id=1, source_target_pairs={{0,4},{2,6},{4,0},{6,2},{1,5},{3,7},{5,1},{7,3},{8,12},{10,14},{12... | collective-permute-start | bytes 196616 | tf_op jit(solution)/shard_map/ppermute | solution.py:35
  82.3 1.9 %backward.1 = (bf16[4,2,32,896]{3,2,1,0:T(8,128)(2,1)S(1)}, bf16[4,2,32,896]{3,2,1,0:T(8,128)(2,1)S(1)}) custom-call(s32[1]{0:T(128)} %bitcast.6.x_ref, f32[2,128,256]{2,1,0:T(8,128)S(1)} %fusion.8.heads_ref, f32[2,256,256]{2,1,0:T(8,128)S(1)} %get-tuple-element.46.key_ref, bf16[2,256,256]{2,1,0:T(8,128)(2,1)S(1)} %get-tuple-element.47.val_ref, ...), custom_call_target="tpu_custom_call" | custom-call | flops 469762048 | bytes 1835008 | tf_op jit(solution)/shard_map/backward/pallas_call | solution.py:209
  89.8 4.6 %all-to-all-start.3 = ((bf16[32,8,512]{2,1,0:T(8,128)(2,1)}), bf16[32,8,512]{2,1,0:T(8,128)(2,1)S(1)}, u32[]{:S(2)}, u32[]{:S(2)}) async-start(bf16[32,8,512]{2,1,0:T(8,128)(2,1)} %output.3), calls=%async_computation.3 | async-start | bytes 524288 | tf_op jit(solution)/shard_map/all_to_all | solution.py:620
  94.6 1.6 %collective-permute-start.22 = (bf16[64,896]{1,0:T(8,128)(2,1)S(1)}, bf16[64,896]{1,0:T(8,128)(2,1)S(1)}, u32[]{:S(2)}, u32[]{:S(2)}) collective-permute-start(bf16[64,896]{1,0:T(8,128)(2,1)S(1)} %bitcast.57), channel_id=1, source_target_pairs={{0,4},{2,6},{4,0},{6,2},{1,5},{3,7},{5,1},{7,3},{8,12},{10,14},{12... | collective-permute-start | bytes 344072 | tf_op jit(solution)/shard_map/ppermute | solution.py:35
  97.0 2.4 %collective-permute-start.21 = (bf16[64,896]{1,0:T(8,128)(2,1)S(1)}, bf16[64,896]{1,0:T(8,128)(2,1)S(1)}, u32[]{:S(2)}, u32[]{:S(2)}) collective-permute-start(bf16[64,896]{1,0:T(8,128)(2,1)S(1)} %bitcast.55), channel_id=1, source_target_pairs={{0,2},{2,0},{4,6},{6,4},{1,3},{3,1},{5,7},{7,5},{8,10},{10,8},{12,... | collective-permute-start | bytes 344072 | tf_op jit(solution)/shard_map/ppermute | solution.py:35
  99.4 2.8 %collective-permute-done.22.t2 = bf16[64,896]{1,0:T(8,128)(2,1)S(1)} collective-permute-done((bf16[64,896]{1,0:T(8,128)(2,1)S(1)}, bf16[64,896]{1,0:T(8,128)(2,1)S(1)}, u32[]{:S(2)}, u32[]{:S(2)}) %collective-permute-start.22) | collective-permute-done | bytes 114720 | tf_op jit(solution)/shard_map/ppermute | solution.py:35
  103.5 4.2 %all-to-all-done.3.piece_ref = bf16[32,8,512]{2,1,0:T(8,128)(2,1)S(1)} async-done(((bf16[32,8,512]{2,1,0:T(8,128)(2,1)}), bf16[32,8,512]{2,1,0:T(8,128)(2,1)S(1)}, u32[]{:S(2)}, u32[]{:S(2)}) %all-to-all-start.3) | async-done | bytes 262176 | tf_op jit(solution)/shard_map/all_to_all | solution.py:620
  107.7 20.4 %all_to_all.26.in_ref = bf16[32,8,768]{2,1,0:T(8,128)(2,1)S(1)} all-to-all(bf16[32,8,768]{2,1,0:T(8,128)(2,1)S(1)} %scan.1), channel_id=1, replica_groups=mesh['segment_0'=8,'segment_1'=4,'tensor_0'=4,'tensor_1'=2] {'segment_0'..., dimensions={0} | all-to-all | bytes 786432 | tf_op jit(solution)/shard_map/all_to_all | solution.py:623
  (67 shorter events, 21.6 us)
Async XLA Ops:
  4.0 30.6 %copy-start.4 = (bf16[896,448]{0,1:T(8,128)(2,1)S(1)}, bf16[896,448]{0,1:T(8,128)(2,1)}, u32[]{:S(2)}) copy-start(bf16[896,448]{0,1:T(8,128)(2,1)} %param.16) | copy-start | bytes 2408452
  26.3 4.2 %collective-permute-start.5 = (bf16[16,896]{1,0:T(8,128)(2,1)S(1)}, bf16[16,896]{1,0:T(8,128)(2,1)S(1)}, u32[]{:S(2)}, u32[]{:S(2)}) collective-permute-start(bf16[16,896]{1,0:T(8,128)(2,1)S(1)} %place.1), channel_id=1, source_target_pairs={{0,6},{2,4},{4,2},{6,0},{1,7},{3,5},{5,3},{7,1},{8,14},{10,12},{12... | collective-permute-start | bytes 86024 | tf_op jit(solution)/shard_map/ppermute | solution.py:35
  27.9 5.4 %collective-permute-start.4 = (bf16[16,896]{1,0:T(8,128)(2,1)S(1)}, bf16[16,896]{1,0:T(8,128)(2,1)S(1)}, u32[]{:S(2)}, u32[]{:S(2)}) collective-permute-start(bf16[16,896]{1,0:T(8,128)(2,1)S(1)} %place.1), channel_id=1, source_target_pairs={{0,4},{2,6},{4,0},{6,2},{1,5},{3,7},{5,1},{7,3},{8,12},{10,14},{12... | collective-permute-start | bytes 86024 | tf_op jit(solution)/shard_map/ppermute | solution.py:35
  29.0 4.3 %collective-permute-start.3 = (bf16[16,896]{1,0:T(8,128)(2,1)S(1)}, bf16[16,896]{1,0:T(8,128)(2,1)S(1)}, u32[]{:S(2)}, u32[]{:S(2)}) collective-permute-start(bf16[16,896]{1,0:T(8,128)(2,1)S(1)} %place.1), channel_id=1, source_target_pairs={{0,2},{2,0},{4,6},{6,4},{1,3},{3,1},{5,7},{7,5},{8,10},{10,8},{12,... | collective-permute-start | bytes 86024 | tf_op jit(solution)/shard_map/ppermute | solution.py:35
  33.3 1.3 %collective-permute-start.6 = (bf16[16,896]{1,0:T(8,128)(2,1)S(1)}, bf16[16,896]{1,0:T(8,128)(2,1)S(1)}, u32[]{:S(2)}, u32[]{:S(2)}) collective-permute-start(bf16[16,896]{1,0:T(8,128)(2,1)S(1)} %pad_maximum_fusion.2), channel_id=1, source_target_pairs={{0,1},{1,0},{2,3},{3,2},{4,5},{5,4},{6,7},{7,6},{8,9},{9,8},{10,11... | collective-permute-start | bytes 86024 | tf_op jit(solution)/shard_map/ppermute | solution.py:35
  35.4 1.2 collective-permute-start.7
  36.6 4.2 %collective-permute-start.10 = (bf16[8,896]{1,0:T(8,128)(2,1)S(1)}, bf16[8,896]{1,0:T(8,128)(2,1)S(1)}, u32[]{:S(2)}, u32[]{:S(2)}) collective-permute-start(bf16[8,896]{1,0:T(8,128)(2,1)S(1)} %add_convert_fusion.4.p0), channel_id=1, source_target_pairs={{0,6},{2,4},{4,2},{6,0},{1,7},{3,5},{5,3},{7,1},{8,14},{10,12},{12... | collective-permute-start | bytes 43016 | tf_op jit(solution)/shard_map/ppermute | solution.py:35
  38.5 5.2 %collective-permute-start.9 = (bf16[8,896]{1,0:T(8,128)(2,1)S(1)}, bf16[8,896]{1,0:T(8,128)(2,1)S(1)}, u32[]{:S(2)}, u32[]{:S(2)}) collective-permute-start(bf16[8,896]{1,0:T(8,128)(2,1)S(1)} %add_convert_fusion.4.p0), channel_id=1, source_target_pairs={{0,4},{2,6},{4,0},{6,2},{1,5},{3,7},{5,1},{7,3},{8,12},{10,14},{12... | collective-permute-start | bytes 43016 | tf_op jit(solution)/shard_map/ppermute | solution.py:35
  40.6 3.7 %collective-permute-start.8 = (bf16[8,896]{1,0:T(8,128)(2,1)S(1)}, bf16[8,896]{1,0:T(8,128)(2,1)S(1)}, u32[]{:S(2)}, u32[]{:S(2)}) collective-permute-start(bf16[8,896]{1,0:T(8,128)(2,1)S(1)} %add_convert_fusion.4.p0), channel_id=1, source_target_pairs={{0,2},{2,0},{4,6},{6,4},{1,3},{3,1},{5,7},{7,5},{8,10},{10,8},{12,... | collective-permute-start | bytes 43016 | tf_op jit(solution)/shard_map/ppermute | solution.py:35
  45.2 19.8 %all-to-all-start.2 = ((bf16[32,8,896]{2,1,0:T(8,128)(2,1)}), bf16[32,8,896]{2,1,0:T(8,128)(2,1)S(1)}, u32[]{:S(2)}, u32[]{:S(2)}) async-start(bf16[32,8,896]{2,1,0:T(8,128)(2,1)} %settle.1), calls=%async_computation.2 | async-start | bytes 917504 | tf_op jit(solution)/shard_map/all_to_all | solution.py:610
  56.2 2.2 %collective-permute-start.12 = (bf16[4,2,128,256]{3,2,1,0:T(8,128)(2,1)}, bf16[4,2,128,256]{3,2,1,0:T(8,128)(2,1)S(1)}, u32[]{:S(2)}, u32[]{:S(2)}) collective-permute-start(bf16[4,2,128,256]{3,2,1,0:T(8,128)(2,1)} %get-tuple-element.42), channel_id=1, source_target_pairs={{0,1},{1,0},{2,3},{3,2},{4,5},{5,4},{6,7},{7,6},{8,9},{9,8},{10,11... | collective-permute-start | bytes 1572872 | tf_op jit(solution)/shard_map/ppermute | solution.py:35
  65.0 10.2 %collective-permute-start.11 = (bf16[256,896]{1,0:T(8,128)(2,1)S(1)}, bf16[256,896]{1,0:T(8,128)(2,1)S(1)}, u32[]{:S(2)}, u32[]{:S(2)}) collective-permute-start(bf16[256,896]{1,0:T(8,128)(2,1)S(1)} %bitcast.43), channel_id=1, source_target_pairs={{0,1},{1,0},{2,3},{3,2},{4,5},{5,4},{6,7},{7,6},{8,9},{9,8},{10,11... | collective-permute-start | bytes 1376264 | tf_op jit(solution)/shard_map/ppermute | solution.py:35
  65.0 6.2 %collective-permute-start.13 = (bf16[2,128,256]{2,1,0:T(8,128)(2,1)S(1)}, bf16[2,128,256]{2,1,0:T(8,128)(2,1)S(1)}, u32[]{:S(2)}, u32[]{:S(2)}) collective-permute-start(bf16[2,128,256]{2,1,0:T(8,128)(2,1)S(1)} %get-tuple-element.58), channel_id=1, source_target_pairs={{0,2},{2,0},{4,6},{6,4},{1,3},{3,1},{5,7},{7,5},{8,10},{10,8},{12,... | collective-permute-start | bytes 393224 | tf_op jit(solution)/shard_map/ppermute | solution.py:35
  66.2 8.4 %collective-permute-start.15 = (bf16[2,128,256]{2,1,0:T(8,128)(2,1)S(1)}, bf16[2,128,256]{2,1,0:T(8,128)(2,1)S(1)}, u32[]{:S(2)}, u32[]{:S(2)}) collective-permute-start(bf16[2,128,256]{2,1,0:T(8,128)(2,1)S(1)} %get-tuple-element.59), channel_id=1, source_target_pairs={{0,6},{2,4},{4,2},{6,0},{1,7},{3,5},{5,3},{7,1},{8,14},{10,12},{12... | collective-permute-start | bytes 393224 | tf_op jit(solution)/shard_map/ppermute | solution.py:35
  67.5 7.2 %collective-permute-start.14 = (bf16[2,128,256]{2,1,0:T(8,128)(2,1)S(1)}, bf16[2,128,256]{2,1,0:T(8,128)(2,1)S(1)}, u32[]{:S(2)}, u32[]{:S(2)}) collective-permute-start(bf16[2,128,256]{2,1,0:T(8,128)(2,1)S(1)} %get-tuple-element.60), channel_id=1, source_target_pairs={{0,4},{2,6},{4,0},{6,2},{1,5},{3,7},{5,1},{7,3},{8,12},{10,14},{12... | collective-permute-start | bytes 393224 | tf_op jit(solution)/shard_map/ppermute | solution.py:35
  78.0 6.3 %collective-permute-start.18 = (bf16[128,256]{1,0:T(8,128)(2,1)S(1)}, bf16[128,256]{1,0:T(8,128)(2,1)S(1)}, u32[]{:S(2)}, u32[]{:S(2)}) collective-permute-start(bf16[128,256]{1,0:T(8,128)(2,1)S(1)} %get-tuple-element.45), channel_id=1, source_target_pairs={{0,6},{2,4},{4,2},{6,0},{1,7},{3,5},{5,3},{7,1},{8,14},{10,12},{12... | collective-permute-start | bytes 196616 | tf_op jit(solution)/shard_map/ppermute | solution.py:35
  79.4 6.3 %collective-permute-start.17 = (bf16[128,256]{1,0:T(8,128)(2,1)S(1)}, bf16[128,256]{1,0:T(8,128)(2,1)S(1)}, u32[]{:S(2)}, u32[]{:S(2)}) collective-permute-start(bf16[128,256]{1,0:T(8,128)(2,1)S(1)} %get-tuple-element.45), channel_id=1, source_target_pairs={{0,4},{2,6},{4,0},{6,2},{1,5},{3,7},{5,1},{7,3},{8,12},{10,14},{12... | collective-permute-start | bytes 196616 | tf_op jit(solution)/shard_map/ppermute | solution.py:35
  82.3 4.3 %collective-permute-start.16 = (bf16[128,256]{1,0:T(8,128)(2,1)S(1)}, bf16[128,256]{1,0:T(8,128)(2,1)S(1)}, u32[]{:S(2)}, u32[]{:S(2)}) collective-permute-start(bf16[128,256]{1,0:T(8,128)(2,1)S(1)} %get-tuple-element.45), channel_id=1, source_target_pairs={{0,2},{2,0},{4,6},{6,4},{1,3},{3,1},{5,7},{7,5},{8,10},{10,8},{12,... | collective-permute-start | bytes 196616 | tf_op jit(solution)/shard_map/ppermute | solution.py:35
  84.2 10.2 %collective-permute-start.20 = (bf16[4,2,32,896]{3,2,1,0:T(8,128)(2,1)S(1)}, bf16[4,2,32,896]{3,2,1,0:T(8,128)(2,1)S(1)}, u32[]{:S(2)}, u32[]{:S(2)}) collective-permute-start(bf16[4,2,32,896]{3,2,1,0:T(8,128)(2,1)S(1)} %get-tuple-element.51), channel_id=1, source_target_pairs={{0,1},{1,0},{2,3},{3,2},{4,5},{5,4},{6,7},{7,6},{8,9},{9,8},{10,11... | collective-permute-start | bytes 1376264 | tf_op jit(solution)/shard_map/ppermute | solution.py:35
  86.6 1.8 %collective-permute-start.19 = (bf16[4,128,256]{2,1,0:T(8,128)(2,1)S(1)}, bf16[4,128,256]{2,1,0:T(8,128)(2,1)S(1)}, u32[]{:S(2)}, u32[]{:S(2)}) collective-permute-start(bf16[4,128,256]{2,1,0:T(8,128)(2,1)S(1)} %pad_maximum_fusion.1.att_ref), channel_id=1, source_target_pairs={{0,1},{1,0},{2,3},{3,2},{4,5},{5,4},{6,7},{7,6},{8,9},{9,8},{10,11... | collective-permute-start | bytes 786440 | tf_op jit(solution)/shard_map/ppermute | solution.py:35
  89.8 17.8 %all-to-all-start.3 = ((bf16[32,8,512]{2,1,0:T(8,128)(2,1)}), bf16[32,8,512]{2,1,0:T(8,128)(2,1)S(1)}, u32[]{:S(2)}, u32[]{:S(2)}) async-start(bf16[32,8,512]{2,1,0:T(8,128)(2,1)} %output.3), calls=%async_computation.3 | async-start | bytes 524288 | tf_op jit(solution)/shard_map/all_to_all | solution.py:620
  94.6 7.6 %collective-permute-start.22 = (bf16[64,896]{1,0:T(8,128)(2,1)S(1)}, bf16[64,896]{1,0:T(8,128)(2,1)S(1)}, u32[]{:S(2)}, u32[]{:S(2)}) collective-permute-start(bf16[64,896]{1,0:T(8,128)(2,1)S(1)} %bitcast.57), channel_id=1, source_target_pairs={{0,4},{2,6},{4,0},{6,2},{1,5},{3,7},{5,1},{7,3},{8,12},{10,14},{12... | collective-permute-start | bytes 344072 | tf_op jit(solution)/shard_map/ppermute | solution.py:35
  96.2 7.1 %collective-permute-start.23 = (bf16[64,896]{1,0:T(8,128)(2,1)S(1)}, bf16[64,896]{1,0:T(8,128)(2,1)S(1)}, u32[]{:S(2)}, u32[]{:S(2)}) collective-permute-start(bf16[64,896]{1,0:T(8,128)(2,1)S(1)} %bitcast.56), channel_id=1, source_target_pairs={{0,6},{2,4},{4,2},{6,0},{1,7},{3,5},{5,3},{7,1},{8,14},{10,12},{12... | collective-permute-start | bytes 344072 | tf_op jit(solution)/shard_map/ppermute | solution.py:35
  97.0 6.3 %collective-permute-start.21 = (bf16[64,896]{1,0:T(8,128)(2,1)S(1)}, bf16[64,896]{1,0:T(8,128)(2,1)S(1)}, u32[]{:S(2)}, u32[]{:S(2)}) collective-permute-start(bf16[64,896]{1,0:T(8,128)(2,1)S(1)} %bitcast.55), channel_id=1, source_target_pairs={{0,2},{2,0},{4,6},{6,4},{1,3},{3,1},{5,7},{7,5},{8,10},{10,8},{12,... | collective-permute-start | bytes 344072 | tf_op jit(solution)/shard_map/ppermute | solution.py:35
  (6 other events, 124.2 us)

commit v2 on v1

--- a/solution.py
+++ b/solution.py
@@ -124,19 +124,28 @@
     )(index, x_in, w_query, grad, w_out)
 
 
-def attend_kernel(own_ref, oth_ref, order_ref, wk_ref, wv_ref, heads_ref, att_ref,
-                  key_ref, val_ref, weight_ref, qhat_ref):
-    wk = wk_ref[...]
-    wv = wv_ref[...]
+def placed_keys(rows_ref, order, wk_ref, wv_ref):
+    rows = rows_ref[...]
+    high, low = halves(dot(rows, wk_ref[...]))
+    value = dot(rows, wv_ref[...]).astype(BF16)
+    return dot(order, high, TN) + dot(order, low, TN), dot(order, value, TN)
+
+
+def attend_own_kernel(own_ref, order_ref, wk_ref, wv_ref, heads_ref, key_ref, val_ref, qhat_ref):
+    key_ref[...], val_ref[...] = placed_keys(own_ref, order_ref[:256, :], wk_ref, wv_ref)
     query = heads_ref[0]
-    query = query * lax.rsqrt(head_mean(query * query) + EPSILON)
-    qhat_ref[...] = query.astype(BF16)
+    qhat_ref[...] = query * lax.rsqrt(head_mean(query * query) + EPSILON)
+
+
+def attend_kernel(oth_ref, order_ref, wk_ref, wv_ref, part_k_ref, part_v_ref, qhat_ref,
+                  att_ref, key_ref, val_ref, weight_ref):
+    keys, values = placed_keys(oth_ref, order_ref[256:, :], wk_ref, wv_ref)
+    keys = keys + part_k_ref[...]
+    values = (values + part_v_ref[...]).astype(BF16)
+    query = qhat_ref[...]
     for span in range(2):
-        places = slice(span * 256, (span + 1) * 256)
-        enc = dot(order_ref[:256, places], own_ref[...], TN)
-        enc = (enc + dot(order_ref[256:, places], oth_ref[...], TN)).astype(BF16)
-        key = dot(enc, wk)
-        value = dot(enc, wv).astype(BF16)
+        key = keys[span * 256 : (span + 1) * 256]
+        value = values[span * 256 : (span + 1) * 256]
         key_ref[span] = key
         val_ref[span] = value
         khat = key * lax.rsqrt(head_mean(key * key) + EPSILON)
@@ -158,22 +167,36 @@
     return pl.BlockSpec(shape, lambda: (0,) * len(shape))
 
 
-def attend(own, oth, places, w_key, w_value, heads):
-    depth = w_key.shape[0]
-    piece = whole((2, 128, 256))
-    shapes = [((128, 256), BF16), ((2, 256, 256), F32), ((2, 256, 256), BF16),
-              ((2, 256, 256), F32), ((128, 256), BF16)]
+def attend_own(own, places, w_key, w_value, heads):
+    operands = (own, places, w_key, w_value, heads)
+    shapes = [((512, 256), F32), ((512, 256), F32), ((128, 256), F32)]
+    return pl.pallas_call(
+        attend_own_kernel,
+        out_shape=[jax.ShapeDtypeStruct(*s) for s in shapes],
+        in_specs=[whole(o.shape) for o in operands],
+        out_specs=[whole(s[0]) for s in shapes],
+        cost_estimate=pl.CostEstimate(
+            flops=4 * 256 * 896 * 256, bytes_accessed=4 * 512 * 896, transcendentals=128
+        ),
+        compiler_params=PARAMS,
+        name="attend_own",
+    )(*operands)
+
+
+def attend(oth, places, w_key, w_value, part_k, part_v, qhat):
+    operands = (oth, places, w_key, w_value, part_k, part_v, qhat)
+    shapes = [((128, 256), BF16), ((2, 256, 256), F32), ((2, 256, 256), BF16), ((2, 256, 256), F32)]
     return pl.pallas_call(
         attend_kernel,
         out_shape=[jax.ShapeDtypeStruct(*s) for s in shapes],
-        in_specs=[whole((256, depth))] * 2 + [whole((512, 512))] + [whole((depth, 256))] * 2 + [piece],
+        in_specs=[whole(o.shape) for o in operands],
         out_specs=[whole(s[0]) for s in shapes],
         cost_estimate=pl.CostEstimate(
-            flops=4 * 512 * depth * 256, bytes_accessed=4 * 512 * depth, transcendentals=131072
+            flops=4 * 512 * 896 * 256, bytes_accessed=4 * 512 * 896, transcendentals=131072
         ),
         compiler_params=PARAMS,
         name="attend",
-    )(own, oth, places, w_key, w_value, heads)
+    )(*operands)
 
 
 def backward_kernel(x_ref, heads_ref, key_ref, val_ref, weight_ref, qhat_ref, wk_ref, wv_ref,
@@ -184,7 +207,7 @@
     for span in range(2):
         rows = slice(span * SPAN, (span + 1) * SPAN)
         d_out = by_head(grad[rows]).astype(BF16)
-        q_rows = by_head(qhat_ref[rows].astype(F32)).astype(BF16)
+        q_rows = by_head(qhat_ref[rows]).astype(BF16)
         weight = weight_ref[span]
         value = val_ref[span]
         d_value = dot(weight.astype(BF16), d_out, TN).astype(BF16)
@@ -611,7 +634,9 @@
     enc_own = enc_own.reshape(256, depth)
     enc_oth = swap(enc_own, C, 1)
 
-    att, *saved = attend(enc_own, enc_oth, places, w_key, w_value, heads)
+    part_k, part_v, qhat = attend_own(enc_own, places, w_key, w_value, heads)
+    att, *saved = attend(enc_oth, places, w_key, w_value, part_k, part_v, qhat)
+    saved.append(qhat)
     atts = jnp.stack([att] + [swap(att, X, k) for k in (1, 2, 3)])
     keep, send = backward(x_index, heads, saved, w_key, w_value)
     atts_other = swap(atts, C, 1)

time: 129 us -> 129 us (level)
  transfers between devices with their start and end apart: 23 -> 23, of which waited for: 16 -> 16; matrix products, arithmetic and copies ran while one was open for 1% -> 1% of each run, Pallas kernels for 9% -> 10%
where the time goes in v2:
time: 129 us
  blocking collectives  42.3 us (33%)
  waiting for transfers between devices  32.5 us (25%)
  starting transfers between devices  31 us (24%)
  Pallas kernels  19.3 us (15%)
  other arithmetic  1.59 us (1%)
  between operations  1.53 us (1%)
    ppermute x21, waiting for transfers between devices, swap(): return lax.ppermute(value, axis, [(i, i ^ k) for i in range(size)])  23 us
    ppermute x21, starting transfers between devices, swap(): return lax.ppermute(value, axis, [(i, i ^ k) for i in range(size)])  22.4 us
    all_to_all x1, blocking collectives, step(): own = lax.all_to_all(found, SEGMENT, 0, 0, tiled=True)  21.9 us
    all_to_all x1, blocking collectives, step(): lax.all_to_all(scan(s_index, x_in, contributions, packed), SEGMENT, 0, 0,...  20.4 us
    pallas_call x1, Pallas kernels, project(): pl.pallas_call(project_kernel, out_shape=[jax.ShapeDtypeStruct(shape, BF1...  6.96 us
    all_to_all x1, waiting for transfers between devices, step(): enc_own = lax.all_to_all(copies, SEGMENT, 0, 0, tiled=True)  5.28 us
    all_to_all x1, starting transfers between devices, step(): contributions = lax.all_to_all(contribution, SEGMENT, 0, 0, tiled=True)  4.56 us
    all_to_all x1, waiting for transfers between devices, step(): contributions = lax.all_to_all(contribution, SEGMENT, 0, 0, tiled=True)  4.16 us
  transfers between devices with their start and end apart: 23, of which 16 were waited for; matrix products, arithmetic and copies ran while one was open for 1% of the time, Pallas kernels for 10%

profile of v2, /device:TPU:2, one launch (start us, length us, event | category | flops | bytes accessed | tf_op | source)
XLA Modules:
  0.0 128.8 jit_solution(17875695335456332143)
XLA Ops:
  0.7 2.0 %lookup.1 = (bf16[32,16,128]{2,1,0:T(8,128)(2,1)S(1)}, bf16[16,128]{1,0:T(8,128)(2,1)S(1)}, s32[1,512]{1,0:T(1,128)S(1)}, s32[8,128]{1,0:T(8,128)S(1)}) custom-call(s32[4]{0:T(128)S(1)} %pad_add_fusion.index_ref, s32[1,512]{1,0:T(1,128)} %bitcast.63, bf16[256,896]{1,0:T(8,128)(2,1)} %table_ref.1), custom_call_target="tpu_custom_call" | custom-call | flops 58720256 | bytes 458752 | tf_op jit(solution)/shard_map/lookup/pallas_call | solution.py:352
  3.9 21.9 %all_to_all.25.piece_ref = bf16[32,16,128]{2,1,0:T(8,128)(2,1)S(1)} all-to-all(bf16[32,16,128]{2,1,0:T(8,128)(2,1)S(1)} %get-tuple-element.38), channel_id=1, replica_groups=mesh['segment_0'=8,'segment_1'=4,'tensor_0'=4,'tensor_1'=2] {'segment_0'..., dimensions={0} | all-to-all | bytes 262144 | tf_op jit(solution)/shard_map/all_to_all | solution.py:611
  26.2 1.5 %collective-permute-start.5 = (bf16[16,896]{1,0:T(8,128)(2,1)S(1)}, bf16[16,896]{1,0:T(8,128)(2,1)S(1)}, u32[]{:S(2)}, u32[]{:S(2)}) collective-permute-start(bf16[16,896]{1,0:T(8,128)(2,1)S(1)} %place.1), channel_id=1, source_target_pairs={{0,6},{2,4},{4,2},{6,0},{1,7},{3,5},{5,3},{7,1},{8,14},{10,12},{12... | collective-permute-start | bytes 86024 | tf_op jit(solution)/shard_map/ppermute | solution.py:35
  28.8 1.5 %collective-permute-start.3 = (bf16[16,896]{1,0:T(8,128)(2,1)S(1)}, bf16[16,896]{1,0:T(8,128)(2,1)S(1)}, u32[]{:S(2)}, u32[]{:S(2)}) collective-permute-start(bf16[16,896]{1,0:T(8,128)(2,1)S(1)} %place.1), channel_id=1, source_target_pairs={{0,2},{2,0},{4,6},{6,4},{1,3},{3,1},{5,7},{7,5},{8,10},{10,8},{12,... | collective-permute-start | bytes 86024 | tf_op jit(solution)/shard_map/ppermute | solution.py:35
  30.4 2.7 %collective-permute-done.4 = bf16[16,896]{1,0:T(8,128)(2,1)S(1)} collective-permute-done((bf16[16,896]{1,0:T(8,128)(2,1)S(1)}, bf16[16,896]{1,0:T(8,128)(2,1)S(1)}, u32[]{:S(2)}, u32[]{:S(2)}) %collective-permute-start.4) | collective-permute-done | bytes 28704 | tf_op jit(solution)/shard_map/ppermute | solution.py:35
  36.5 1.8 %collective-permute-start.10 = (bf16[8,896]{1,0:T(8,128)(2,1)S(1)}, bf16[8,896]{1,0:T(8,128)(2,1)S(1)}, u32[]{:S(2)}, u32[]{:S(2)}) collective-permute-start(bf16[8,896]{1,0:T(8,128)(2,1)S(1)} %add_convert_fusion.4.p0), channel_id=1, source_target_pairs={{0,6},{2,4},{4,2},{6,0},{1,7},{3,5},{5,3},{7,1},{8,14},{10,12},{12... | collective-permute-start | bytes 43016 | tf_op jit(solution)/shard_map/ppermute | solution.py:35
  38.3 2.1 %collective-permute-start.9 = (bf16[8,896]{1,0:T(8,128)(2,1)S(1)}, bf16[8,896]{1,0:T(8,128)(2,1)S(1)}, u32[]{:S(2)}, u32[]{:S(2)}) collective-permute-start(bf16[8,896]{1,0:T(8,128)(2,1)S(1)} %add_convert_fusion.4.p0), channel_id=1, source_target_pairs={{0,4},{2,6},{4,0},{6,2},{1,5},{3,7},{5,1},{7,3},{8,12},{10,14},{12... | collective-permute-start | bytes 43016 | tf_op jit(solution)/shard_map/ppermute | solution.py:35
  40.6 2.9 %collective-permute-done.9.p2 = bf16[8,896]{1,0:T(8,128)(2,1)S(1)} collective-permute-done((bf16[8,896]{1,0:T(8,128)(2,1)S(1)}, bf16[8,896]{1,0:T(8,128)(2,1)S(1)}, u32[]{:S(2)}, u32[]{:S(2)}) %collective-permute-start.9) | collective-permute-done | bytes 14368 | tf_op jit(solution)/shard_map/ppermute | solution.py:35
  45.0 4.1 %all-to-all-start.2 = ((bf16[32,8,896]{2,1,0:T(8,128)(2,1)}), bf16[32,8,896]{2,1,0:T(8,128)(2,1)S(1)}, u32[]{:S(2)}, u32[]{:S(2)}) async-start(bf16[32,8,896]{2,1,0:T(8,128)(2,1)} %settle.1), calls=%async_computation.2 | async-start | bytes 917504 | tf_op jit(solution)/shard_map/all_to_all | solution.py:633
  49.1 7.0 %project.1 = (bf16[4,2,128,256]{3,2,1,0:T(8,128)(2,1)}, bf16[4,2,128,256]{3,2,1,0:T(8,128)(2,1)}) custom-call(s32[1]{0:T(128)} %bitcast.3.index_ref, bf16[128,1024]{1,0:T(8,128)(2,1)} %x_ref.1, bf16[1024,2048]{1,0:T(8,128)(2,1)} %bitcast.55, bf16[128,1024]{1,0:T(8,128)(2,1)} %bitcast.56, bf16[2048,1024]{1,0:T(8,128)(2,1)} %bitcast.40), custom_call_target="tpu_custom_call" | custom-call | flops 1073741824 | bytes 8388608 | tf_op jit(solution)/shard_map/project/pallas_call | solution.py:105
  56.2 2.1 %collective-permute-done.12 = bf16[4,2,128,256]{3,2,1,0:T(8,128)(2,1)S(1)} collective-permute-done((bf16[4,2,128,256]{3,2,1,0:T(8,128)(2,1)}, bf16[4,2,128,256]{3,2,1,0:T(8,128)(2,1)S(1)}, u32[]{:S(2)}, u32[]{:S(2)}) %collective-permute-start.12) | collective-permute-done | bytes 524320 | tf_op jit(solution)/shard_map/ppermute | solution.py:35
  59.5 5.3 %all-to-all-done.2 = bf16[32,8,896]{2,1,0:T(8,128)(2,1)S(1)} async-done(((bf16[32,8,896]{2,1,0:T(8,128)(2,1)}), bf16[32,8,896]{2,1,0:T(8,128)(2,1)S(1)}, u32[]{:S(2)}, u32[]{:S(2)}) %all-to-all-start.2) | async-done | bytes 458784 | tf_op jit(solution)/shard_map/all_to_all | solution.py:633
  67.3 1.7 %collective-permute-start.14 = (bf16[2,128,256]{2,1,0:T(8,128)(2,1)S(1)}, bf16[2,128,256]{2,1,0:T(8,128)(2,1)S(1)}, u32[]{:S(2)}, u32[]{:S(2)}) collective-permute-start(bf16[2,128,256]{2,1,0:T(8,128)(2,1)S(1)} %get-tuple-element.64), channel_id=1, source_target_pairs={{0,4},{2,6},{4,0},{6,2},{1,5},{3,7},{5,1},{7,3},{8,12},{10,14},{12... | collective-permute-start | bytes 393224 | tf_op jit(solution)/shard_map/ppermute | solution.py:35
  69.0 2.0 %collective-permute-done.13 = bf16[2,128,256]{2,1,0:T(8,128)(2,1)S(1)} collective-permute-done((bf16[2,128,256]{2,1,0:T(8,128)(2,1)S(1)}, bf16[2,128,256]{2,1,0:T(8,128)(2,1)S(1)}, u32[]{:S(2)}, u32[]{:S(2)}) %collective-permute-start.13) | collective-permute-done | bytes 131104 | tf_op jit(solution)/shard_map/ppermute | solution.py:35
  71.0 3.5 %collective-permute-done.15 = bf16[2,128,256]{2,1,0:T(8,128)(2,1)S(1)} collective-permute-done((bf16[2,128,256]{2,1,0:T(8,128)(2,1)S(1)}, bf16[2,128,256]{2,1,0:T(8,128)(2,1)S(1)}, u32[]{:S(2)}, u32[]{:S(2)}) %collective-permute-start.15) | collective-permute-done | bytes 131104 | tf_op jit(solution)/shard_map/ppermute | solution.py:35
  75.9 2.1 %attend.1 = (bf16[128,256]{1,0:T(8,128)(2,1)S(1)}, f32[2,256,256]{2,1,0:T(8,128)S(1)}, bf16[2,256,256]{2,1,0:T(8,128)(2,1)S(1)}, f32[2,256,256]{2,1,0:T(8,128)S(1)}) custom-call(bf16[256,896]{1,0:T(8,128)(2,1)S(1)} %collective-permute-done.11.oth_ref, bf16[512,512]{1,0:T(8,128)(2,1)S(1)} %order.1.order_ref, bf16[896,256]{1,0:T(8,128)(2,1)S(1)} %bitcast.44, ...), custom_call_target="tpu_custom_call" | custom-call | flops 469762048 | bytes 1835008 | tf_op jit(solution)/shard_map/attend/pallas_call | solution.py:189
  79.3 2.9 %collective-permute-start.17 = (bf16[128,256]{1,0:T(8,128)(2,1)S(1)}, bf16[128,256]{1,0:T(8,128)(2,1)S(1)}, u32[]{:S(2)}, u32[]{:S(2)}) collective-permute-start(bf16[128,256]{1,0:T(8,128)(2,1)S(1)} %get-tuple-element.50), channel_id=1, source_target_pairs={{0,4},{2,6},{4,0},{6,2},{1,5},{3,7},{5,1},{7,3},{8,12},{10,14},{12... | collective-permute-start | bytes 196616 | tf_op jit(solution)/shard_map/ppermute | solution.py:35
  82.3 1.9 %backward.1 = (bf16[4,2,32,896]{3,2,1,0:T(8,128)(2,1)S(1)}, bf16[4,2,32,896]{3,2,1,0:T(8,128)(2,1)S(1)}) custom-call(s32[1]{0:T(128)} %bitcast.6.x_ref, f32[2,128,256]{2,1,0:T(8,128)S(1)} %fusion.8.heads_ref, f32[2,256,256]{2,1,0:T(8,128)S(1)} %get-tuple-element.51.key_ref, bf16[2,256,256]{2,1,0:T(8,128)(2,1)S(1)} %get-tuple-element.52.val_ref, ...), custom_call_target="tpu_custom_call" | custom-call | flops 469762048 | bytes 1835008 | tf_op jit(solution)/shard_map/backward/pallas_call | solution.py:232
  89.8 4.6 %all-to-all-start.3 = ((bf16[32,8,512]{2,1,0:T(8,128)(2,1)}), bf16[32,8,512]{2,1,0:T(8,128)(2,1)S(1)}, u32[]{:S(2)}, u32[]{:S(2)}) async-start(bf16[32,8,512]{2,1,0:T(8,128)(2,1)} %output.3), calls=%async_computation.3 | async-start | bytes 524288 | tf_op jit(solution)/shard_map/all_to_all | solution.py:645
  94.6 1.6 %collective-permute-start.22 = (bf16[64,896]{1,0:T(8,128)(2,1)S(1)}, bf16[64,896]{1,0:T(8,128)(2,1)S(1)}, u32[]{:S(2)}, u32[]{:S(2)}) collective-permute-start(bf16[64,896]{1,0:T(8,128)(2,1)S(1)} %bitcast.59), channel_id=1, source_target_pairs={{0,4},{2,6},{4,0},{6,2},{1,5},{3,7},{5,1},{7,3},{8,12},{10,14},{12... | collective-permute-start | bytes 344072 | tf_op jit(solution)/shard_map/ppermute | solution.py:35
  96.9 2.4 %collective-permute-start.21 = (bf16[64,896]{1,0:T(8,128)(2,1)S(1)}, bf16[64,896]{1,0:T(8,128)(2,1)S(1)}, u32[]{:S(2)}, u32[]{:S(2)}) collective-permute-start(bf16[64,896]{1,0:T(8,128)(2,1)S(1)} %bitcast.57), channel_id=1, source_target_pairs={{0,2},{2,0},{4,6},{6,4},{1,3},{3,1},{5,7},{7,5},{8,10},{10,8},{12,... | collective-permute-start | bytes 344072 | tf_op jit(solution)/shard_map/ppermute | solution.py:35
  99.4 2.8 %collective-permute-done.22.t2 = bf16[64,896]{1,0:T(8,128)(2,1)S(1)} collective-permute-done((bf16[64,896]{1,0:T(8,128)(2,1)S(1)}, bf16[64,896]{1,0:T(8,128)(2,1)S(1)}, u32[]{:S(2)}, u32[]{:S(2)}) %collective-permute-start.22) | collective-permute-done | bytes 114720 | tf_op jit(solution)/shard_map/ppermute | solution.py:35
  103.5 4.2 %all-to-all-done.3.piece_ref = bf16[32,8,512]{2,1,0:T(8,128)(2,1)S(1)} async-done(((bf16[32,8,512]{2,1,0:T(8,128)(2,1)}), bf16[32,8,512]{2,1,0:T(8,128)(2,1)S(1)}, u32[]{:S(2)}, u32[]{:S(2)}) %all-to-all-start.3) | async-done | bytes 262176 | tf_op jit(solution)/shard_map/all_to_all | solution.py:645
  107.7 20.4 %all_to_all.26.in_ref = bf16[32,8,768]{2,1,0:T(8,128)(2,1)S(1)} all-to-all(bf16[32,8,768]{2,1,0:T(8,128)(2,1)S(1)} %scan.1), channel_id=1, replica_groups=mesh['segment_0'=8,'segment_1'=4,'tensor_0'=4,'tensor_1'=2] {'segment_0'..., dimensions={0} | all-to-all | bytes 786432 | tf_op jit(solution)/shard_map/all_to_all | solution.py:648
  (68 shorter events, 22.3 us)
Async XLA Ops:
  3.9 30.6 %copy-start.4 = (bf16[896,448]{0,1:T(8,128)(2,1)S(1)}, bf16[896,448]{0,1:T(8,128)(2,1)}, u32[]{:S(2)}) copy-start(bf16[896,448]{0,1:T(8,128)(2,1)} %param.16) | copy-start | bytes 2408452
  26.2 4.2 %collective-permute-start.5 = (bf16[16,896]{1,0:T(8,128)(2,1)S(1)}, bf16[16,896]{1,0:T(8,128)(2,1)S(1)}, u32[]{:S(2)}, u32[]{:S(2)}) collective-permute-start(bf16[16,896]{1,0:T(8,128)(2,1)S(1)} %place.1), channel_id=1, source_target_pairs={{0,6},{2,4},{4,2},{6,0},{1,7},{3,5},{5,3},{7,1},{8,14},{10,12},{12... | collective-permute-start | bytes 86024 | tf_op jit(solution)/shard_map/ppermute | solution.py:35
  27.7 5.4 %collective-permute-start.4 = (bf16[16,896]{1,0:T(8,128)(2,1)S(1)}, bf16[16,896]{1,0:T(8,128)(2,1)S(1)}, u32[]{:S(2)}, u32[]{:S(2)}) collective-permute-start(bf16[16,896]{1,0:T(8,128)(2,1)S(1)} %place.1), channel_id=1, source_target_pairs={{0,4},{2,6},{4,0},{6,2},{1,5},{3,7},{5,1},{7,3},{8,12},{10,14},{12... | collective-permute-start | bytes 86024 | tf_op jit(solution)/shard_map/ppermute | solution.py:35
  28.8 4.3 %collective-permute-start.3 = (bf16[16,896]{1,0:T(8,128)(2,1)S(1)}, bf16[16,896]{1,0:T(8,128)(2,1)S(1)}, u32[]{:S(2)}, u32[]{:S(2)}) collective-permute-start(bf16[16,896]{1,0:T(8,128)(2,1)S(1)} %place.1), channel_id=1, source_target_pairs={{0,2},{2,0},{4,6},{6,4},{1,3},{3,1},{5,7},{7,5},{8,10},{10,8},{12,... | collective-permute-start | bytes 86024 | tf_op jit(solution)/shard_map/ppermute | solution.py:35
  33.1 1.3 %collective-permute-start.6 = (bf16[16,896]{1,0:T(8,128)(2,1)S(1)}, bf16[16,896]{1,0:T(8,128)(2,1)S(1)}, u32[]{:S(2)}, u32[]{:S(2)}) collective-permute-start(bf16[16,896]{1,0:T(8,128)(2,1)S(1)} %pad_maximum_fusion.2), channel_id=1, source_target_pairs={{0,1},{1,0},{2,3},{3,2},{4,5},{5,4},{6,7},{7,6},{8,9},{9,8},{10,11... | collective-permute-start | bytes 86024 | tf_op jit(solution)/shard_map/ppermute | solution.py:35
  35.2 1.2 collective-permute-start.7
  36.5 4.2 %collective-permute-start.10 = (bf16[8,896]{1,0:T(8,128)(2,1)S(1)}, bf16[8,896]{1,0:T(8,128)(2,1)S(1)}, u32[]{:S(2)}, u32[]{:S(2)}) collective-permute-start(bf16[8,896]{1,0:T(8,128)(2,1)S(1)} %add_convert_fusion.4.p0), channel_id=1, source_target_pairs={{0,6},{2,4},{4,2},{6,0},{1,7},{3,5},{5,3},{7,1},{8,14},{10,12},{12... | collective-permute-start | bytes 43016 | tf_op jit(solution)/shard_map/ppermute | solution.py:35
  38.3 5.2 %collective-permute-start.9 = (bf16[8,896]{1,0:T(8,128)(2,1)S(1)}, bf16[8,896]{1,0:T(8,128)(2,1)S(1)}, u32[]{:S(2)}, u32[]{:S(2)}) collective-permute-start(bf16[8,896]{1,0:T(8,128)(2,1)S(1)} %add_convert_fusion.4.p0), channel_id=1, source_target_pairs={{0,4},{2,6},{4,0},{6,2},{1,5},{3,7},{5,1},{7,3},{8,12},{10,14},{12... | collective-permute-start | bytes 43016 | tf_op jit(solution)/shard_map/ppermute | solution.py:35
  40.4 3.7 %collective-permute-start.8 = (bf16[8,896]{1,0:T(8,128)(2,1)S(1)}, bf16[8,896]{1,0:T(8,128)(2,1)S(1)}, u32[]{:S(2)}, u32[]{:S(2)}) collective-permute-start(bf16[8,896]{1,0:T(8,128)(2,1)S(1)} %add_convert_fusion.4.p0), channel_id=1, source_target_pairs={{0,2},{2,0},{4,6},{6,4},{1,3},{3,1},{5,7},{7,5},{8,10},{10,8},{12,... | collective-permute-start | bytes 43016 | tf_op jit(solution)/shard_map/ppermute | solution.py:35
  45.0 19.8 %all-to-all-start.2 = ((bf16[32,8,896]{2,1,0:T(8,128)(2,1)}), bf16[32,8,896]{2,1,0:T(8,128)(2,1)S(1)}, u32[]{:S(2)}, u32[]{:S(2)}) async-start(bf16[32,8,896]{2,1,0:T(8,128)(2,1)} %settle.1), calls=%async_computation.2 | async-start | bytes 917504 | tf_op jit(solution)/shard_map/all_to_all | solution.py:633
  56.1 2.2 %collective-permute-start.12 = (bf16[4,2,128,256]{3,2,1,0:T(8,128)(2,1)}, bf16[4,2,128,256]{3,2,1,0:T(8,128)(2,1)S(1)}, u32[]{:S(2)}, u32[]{:S(2)}) collective-permute-start(bf16[4,2,128,256]{3,2,1,0:T(8,128)(2,1)} %get-tuple-element.44), channel_id=1, source_target_pairs={{0,1},{1,0},{2,3},{3,2},{4,5},{5,4},{6,7},{7,6},{8,9},{9,8},{10,11... | collective-permute-start | bytes 1572872 | tf_op jit(solution)/shard_map/ppermute | solution.py:35
  64.8 11.1 %collective-permute-start.11 = (bf16[256,896]{1,0:T(8,128)(2,1)S(1)}, bf16[256,896]{1,0:T(8,128)(2,1)S(1)}, u32[]{:S(2)}, u32[]{:S(2)}) collective-permute-start(bf16[256,896]{1,0:T(8,128)(2,1)S(1)} %bitcast.49), channel_id=1, source_target_pairs={{0,1},{1,0},{2,3},{3,2},{4,5},{5,4},{6,7},{7,6},{8,9},{9,8},{10,11... | collective-permute-start | bytes 1376264 | tf_op jit(solution)/shard_map/ppermute | solution.py:35
  64.8 6.2 %collective-permute-start.13 = (bf16[2,128,256]{2,1,0:T(8,128)(2,1)S(1)}, bf16[2,128,256]{2,1,0:T(8,128)(2,1)S(1)}, u32[]{:S(2)}, u32[]{:S(2)}) collective-permute-start(bf16[2,128,256]{2,1,0:T(8,128)(2,1)S(1)} %get-tuple-element.62), channel_id=1, source_target_pairs={{0,2},{2,0},{4,6},{6,4},{1,3},{3,1},{5,7},{7,5},{8,10},{10,8},{12,... | collective-permute-start | bytes 393224 | tf_op jit(solution)/shard_map/ppermute | solution.py:35
  66.0 8.4 %collective-permute-start.15 = (bf16[2,128,256]{2,1,0:T(8,128)(2,1)S(1)}, bf16[2,128,256]{2,1,0:T(8,128)(2,1)S(1)}, u32[]{:S(2)}, u32[]{:S(2)}) collective-permute-start(bf16[2,128,256]{2,1,0:T(8,128)(2,1)S(1)} %get-tuple-element.63), channel_id=1, source_target_pairs={{0,6},{2,4},{4,2},{6,0},{1,7},{3,5},{5,3},{7,1},{8,14},{10,12},{12... | collective-permute-start | bytes 393224 | tf_op jit(solution)/shard_map/ppermute | solution.py:35
  67.3 7.2 %collective-permute-start.14 = (bf16[2,128,256]{2,1,0:T(8,128)(2,1)S(1)}, bf16[2,128,256]{2,1,0:T(8,128)(2,1)S(1)}, u32[]{:S(2)}, u32[]{:S(2)}) collective-permute-start(bf16[2,128,256]{2,1,0:T(8,128)(2,1)S(1)} %get-tuple-element.64), channel_id=1, source_target_pairs={{0,4},{2,6},{4,0},{6,2},{1,5},{3,7},{5,1},{7,3},{8,12},{10,14},{12... | collective-permute-start | bytes 393224 | tf_op jit(solution)/shard_map/ppermute | solution.py:35
  78.0 6.3 %collective-permute-start.18 = (bf16[128,256]{1,0:T(8,128)(2,1)S(1)}, bf16[128,256]{1,0:T(8,128)(2,1)S(1)}, u32[]{:S(2)}, u32[]{:S(2)}) collective-permute-start(bf16[128,256]{1,0:T(8,128)(2,1)S(1)} %get-tuple-element.50), channel_id=1, source_target_pairs={{0,6},{2,4},{4,2},{6,0},{1,7},{3,5},{5,3},{7,1},{8,14},{10,12},{12... | collective-permute-start | bytes 196616 | tf_op jit(solution)/shard_map/ppermute | solution.py:35
  79.3 6.3 %collective-permute-start.17 = (bf16[128,256]{1,0:T(8,128)(2,1)S(1)}, bf16[128,256]{1,0:T(8,128)(2,1)S(1)}, u32[]{:S(2)}, u32[]{:S(2)}) collective-permute-start(bf16[128,256]{1,0:T(8,128)(2,1)S(1)} %get-tuple-element.50), channel_id=1, source_target_pairs={{0,4},{2,6},{4,0},{6,2},{1,5},{3,7},{5,1},{7,3},{8,12},{10,14},{12... | collective-permute-start | bytes 196616 | tf_op jit(solution)/shard_map/ppermute | solution.py:35
  82.3 4.3 %collective-permute-start.16 = (bf16[128,256]{1,0:T(8,128)(2,1)S(1)}, bf16[128,256]{1,0:T(8,128)(2,1)S(1)}, u32[]{:S(2)}, u32[]{:S(2)}) collective-permute-start(bf16[128,256]{1,0:T(8,128)(2,1)S(1)} %get-tuple-element.50), channel_id=1, source_target_pairs={{0,2},{2,0},{4,6},{6,4},{1,3},{3,1},{5,7},{7,5},{8,10},{10,8},{12,... | collective-permute-start | bytes 196616 | tf_op jit(solution)/shard_map/ppermute | solution.py:35
  84.2 10.2 %collective-permute-start.20 = (bf16[4,2,32,896]{3,2,1,0:T(8,128)(2,1)S(1)}, bf16[4,2,32,896]{3,2,1,0:T(8,128)(2,1)S(1)}, u32[]{:S(2)}, u32[]{:S(2)}) collective-permute-start(bf16[4,2,32,896]{3,2,1,0:T(8,128)(2,1)S(1)} %get-tuple-element.55), channel_id=1, source_target_pairs={{0,1},{1,0},{2,3},{3,2},{4,5},{5,4},{6,7},{7,6},{8,9},{9,8},{10,11... | collective-permute-start | bytes 1376264 | tf_op jit(solution)/shard_map/ppermute | solution.py:35
  86.6 1.8 %collective-permute-start.19 = (bf16[4,128,256]{2,1,0:T(8,128)(2,1)S(1)}, bf16[4,128,256]{2,1,0:T(8,128)(2,1)S(1)}, u32[]{:S(2)}, u32[]{:S(2)}) collective-permute-start(bf16[4,128,256]{2,1,0:T(8,128)(2,1)S(1)} %pad_maximum_fusion.1.att_ref), channel_id=1, source_target_pairs={{0,1},{1,0},{2,3},{3,2},{4,5},{5,4},{6,7},{7,6},{8,9},{9,8},{10,11... | collective-permute-start | bytes 786440 | tf_op jit(solution)/shard_map/ppermute | solution.py:35
  89.8 17.8 %all-to-all-start.3 = ((bf16[32,8,512]{2,1,0:T(8,128)(2,1)}), bf16[32,8,512]{2,1,0:T(8,128)(2,1)S(1)}, u32[]{:S(2)}, u32[]{:S(2)}) async-start(bf16[32,8,512]{2,1,0:T(8,128)(2,1)} %output.3), calls=%async_computation.3 | async-start | bytes 524288 | tf_op jit(solution)/shard_map/all_to_all | solution.py:645
  94.6 7.6 %collective-permute-start.22 = (bf16[64,896]{1,0:T(8,128)(2,1)S(1)}, bf16[64,896]{1,0:T(8,128)(2,1)S(1)}, u32[]{:S(2)}, u32[]{:S(2)}) collective-permute-start(bf16[64,896]{1,0:T(8,128)(2,1)S(1)} %bitcast.59), channel_id=1, source_target_pairs={{0,4},{2,6},{4,0},{6,2},{1,5},{3,7},{5,1},{7,3},{8,12},{10,14},{12... | collective-permute-start | bytes 344072 | tf_op jit(solution)/shard_map/ppermute | solution.py:35
  96.2 7.1 %collective-permute-start.23 = (bf16[64,896]{1,0:T(8,128)(2,1)S(1)}, bf16[64,896]{1,0:T(8,128)(2,1)S(1)}, u32[]{:S(2)}, u32[]{:S(2)}) collective-permute-start(bf16[64,896]{1,0:T(8,128)(2,1)S(1)} %bitcast.58), channel_id=1, source_target_pairs={{0,6},{2,4},{4,2},{6,0},{1,7},{3,5},{5,3},{7,1},{8,14},{10,12},{12... | collective-permute-start | bytes 344072 | tf_op jit(solution)/shard_map/ppermute | solution.py:35
  96.9 6.3 %collective-permute-start.21 = (bf16[64,896]{1,0:T(8,128)(2,1)S(1)}, bf16[64,896]{1,0:T(8,128)(2,1)S(1)}, u32[]{:S(2)}, u32[]{:S(2)}) collective-permute-start(bf16[64,896]{1,0:T(8,128)(2,1)S(1)} %bitcast.57), channel_id=1, source_target_pairs={{0,2},{2,0},{4,6},{6,4},{1,3},{3,1},{5,7},{7,5},{8,10},{10,8},{12,... | collective-permute-start | bytes 344072 | tf_op jit(solution)/shard_map/ppermute | solution.py:35
  (6 other events, 123.5 us)
